TPU v7x, 32 devices: a whole 2x2x4 slice. The times are simulated.
32 devices in a mesh: grp: 2 (over x), row: 8 (over z, y), col: 2 (over core).
Axes of the slice: x: 2, y: 2, z: 4, core: 2. Of those that a mesh axis runs over, the one named last changes fastest.
Arguments:
- density: bfloat16 [1024, 32, 128], P(('grp', 'row', 'col')), parts along dimension 0, may hold values from -6 to 6
- leaf_target: int32 [1024], P(('grp', 'row', 'col')), parts along dimension 0, may hold values from 0 to 511, as said below
- geometry: float32 [6, 131072], P(None, ('grp', 'row', 'col')), parts along dimension 1, may hold values from -6 to 6
- near_list: int32 [1024, 16], P(('grp', 'row', 'col')), parts along dimension 0, may hold values from -1 to 511, as said below
- far_list: int32 [1024, 16], P(('grp', 'row', 'col')), parts along dimension 0, may hold values from -1 to 511, as said below
- node_list: int32 [128, 32], P(('grp', 'row', 'col')), parts along dimension 0, may hold values from -1 to 63, as said below
- basis_in: bfloat16 [1024, 64, 128], P(('grp', 'row', 'col')), parts along dimension 0, may hold values from -0.5 to 0.5
- basis_out: bfloat16 [1024, 64, 128], P(('grp', 'row', 'col')), parts along dimension 0, may hold values from -0.75 to 0.75
- transfer: bfloat16 [128, 64, 512], P(('grp', 'row', 'col')), parts along dimension 0, may hold values from -0.25 to 0.25
- node_points: float32 [3, 8192], P(None, 'grp'), parts along dimension 1, may hold values from -6 to 6
Outputs:
- potential: bfloat16 [1024, 32, 128], P(('grp', 'row', 'col')), parts along dimension 0
There are 2 independent parts, one for each index of `grp`. A program takes and returns all parts, laid end to end along the dimension named above; each array names one. Nothing has to cross between parts.
Inputs may be any that keep to these rules, and one draw needn't show every extreme that they name: `leaf_target`: A permutation of the tree positions; of the 32 slab leaves of one device, exactly 2 go to the block of 32 tree positions of each device. `near_list`: row t holds t in slot 0; every other slot holds either -1 or a leaf other than t within 16 of t, the leaves of a row distinct; a -1 may stand in any slot after slot 0, also between leaves. `far_list`: every slot of row t holds either -1 or a leaf within 16 of t that is neither t nor in row t of near_list, the leaves of a row distinct; a -1 may stand in any slot, also between leaves. `node_list`: row p holds distinct nodes that differ from p by more than 2, then -1 in the unused slots.
All inputs are finite; a program needn't handle non-finite values.
Results may differ from a plain program's by a relative error of at most 0.0053.
Values may be sent and summed in bfloat16 or wider, within the bound.
No kernel may reach another device: no remote copies, remote signals or barrier semaphores. Data moves between devices by JAX's collectives and lax.ppermute only.
A program may use at most 64 MiB of HBM per device.

v0:
```python
import math

import jax
import jax.numpy as jnp
from jax import lax
from jax.experimental import pallas as pl
from jax.experimental.pallas import tpu as pltpu
from jax.sharding import PartitionSpec as P

REACH = 16
AXES = ("row", "col")

smoothing = 0.1
inv_four_pi = 0.25 / math.pi
grid_step = 16.0
UNROLL = 8
LEAD = UNROLL
bf16 = jnp.bfloat16
f32 = jnp.float32


def split3(x):
    first = x.astype(bf16).astype(f32)
    rest = x - first
    second = rest.astype(bf16).astype(f32)
    third = (rest - second).astype(bf16).astype(f32)
    return first, second, third


def iota(shape, axis):
    return lax.broadcasted_iota(jnp.int32, shape, axis)


def dot(a, b):
    return lax.dot_general(a, b, (((1,), (0,)), ((), ())), preferred_element_type=f32)


def dot_t(a, b):
    return lax.dot_general(a, b, (((1,), (1,)), ((), ())), preferred_element_type=f32)


class Features:
    def __init__(self, g):
        self.shape = g.shape
        self.row = row = iota(g.shape, 0)
        point = row < 3
        c = jnp.where(point, g, 0.0)
        self.whole = whole = jnp.floor(c * grid_step + 0.5) * (1.0 / grid_step)
        part = c - whole
        self.part = split3(part)
        m = jnp.where(point, 0.0, g) * inv_four_pi
        self.m = split3(m)
        norm = jnp.sum(whole * whole, axis=0, keepdims=True)
        self.norm_hi = jnp.floor(norm)
        self.norm_lo = norm - self.norm_hi
        self.cross = jnp.sum(part * (2.0 * whole + part), axis=0, keepdims=True)
        self.q = split3(jnp.sum(m * pltpu.roll(c, 3, 0), axis=0, keepdims=True))
        self.low = {}

    def moved(self, x):
        if id(x) not in self.low:
            self.low[id(x)] = pltpu.roll(x, 3, 0)
        return self.low[id(x)]

    def tile(self, upper, lower, six, seven):
        row = self.row
        x = jnp.where(row < 3, upper, 0.0)
        if lower is not None:
            x = jnp.where(row < 3, upper, jnp.where(row < 6, lower, 0.0))
        if six is not None:
            x = jnp.where(row == 6, six, x)
        if seven is not None:
            x = jnp.where(row == 7, seven, x)
        return x

    def first(self, points, three, four, five, six):
        row = self.row
        x = jnp.where(row == 3, three, jnp.where(row == 4, four, 0.0))
        x = jnp.where(row == 5, five, jnp.where(row == 6, six, x))
        return jnp.where(row < 3, points, x)

    def zeros(self, rows):
        return jnp.zeros((rows, self.shape[1]), f32)

    def source_square(self):
        w, (p0, p1, p2) = self.whole, self.part
        c0, c1, c2 = split3(self.cross)
        move = self.moved
        return [
            self.first(w, self.norm_hi, self.norm_lo, 1.0, 1.0),
            self.tile(w, move(w), 1.0, 1.0),
            self.tile(w, move(p0), 1.0, c0),
            self.tile(p1, move(p2), c1, c2),
            self.tile(p0, move(p1), None, None),
            self.tile(p0, None, None, None),
            self.zeros(16),
        ]

    def source_normal(self):
        m0, m1, m2 = self.m
        u0, u1, u2 = (pltpu.roll(x, 5, 0) for x in self.m)
        q0, q1, q2 = self.q
        return [
            self.tile(u0, m1, q0, q1),
            self.tile(u2, m0, q2, None),
            self.tile(u0, m0, None, None),
            self.tile(u1, m1, None, None),
            self.tile(u2, None, None, None),
            self.zeros(24),
        ]

    def target_square(self):
        w, part = -2.0 * self.whole, [-2.0 * p for p in self.part]
        p0, p1, p2 = part
        c0, c1, c2 = split3(self.cross + smoothing * smoothing)
        w3, p03, p13 = (pltpu.roll(x, 3, 0) for x in (w, p0, p1))
        return [
            self.first(w, 1.0, 1.0, self.norm_hi, self.norm_lo),
            self.tile(p0, p13, c0, c1),
            self.tile(p2, w3, c2, 1.0),
            self.tile(w, w3, 1.0, 1.0),
            self.tile(p0, p03, None, None),
            self.tile(p1, None, None, None),
            self.zeros(16),
        ]

    def target_normal(self):
        w, (p0, p1, p2) = self.whole, self.part
        move = self.moved
        return [
            self.tile(w, move(w), -1.0, -1.0),
            self.tile(w, move(p0), -1.0, None),
            self.tile(p1, move(p2), None, None),
            self.tile(p0, move(p1), None, None),
            self.tile(p0, None, None, None),
            self.zeros(24),
        ]


def sources(f):
    x = jnp.concatenate(f.source_square() + f.source_normal(), axis=0).T
    top = x[:64]
    left = iota(top.shape, 1) < 64
    return x.astype(bf16), jnp.where(left, top, pltpu.roll(top, 64, 1)).astype(bf16)


def point_sources(f):
    x = f.source_square()
    return jnp.concatenate(x + x, axis=0).T.astype(bf16)


def halves(x):
    left = iota(x.shape, 1) < 64
    a = jnp.where(left, x, 0.0)
    b = jnp.where(left, 0.0, x)
    return (a, pltpu.roll(a, 64, 1)), (pltpu.roll(b, 64, 1), b)


def pair_weights(square):
    return [jnp.concatenate(x, axis=0).astype(bf16) for x in halves(jnp.concatenate(square, axis=0))]


def compact(entries, first, dead):
    slots, targets = entries.shape
    place = iota(entries.shape, 0)
    out = jnp.full(entries.shape, dead, jnp.int32)
    count = jnp.zeros((1, targets), jnp.int32)
    for k in range(slots):
        e = entries[k : k + 1]
        live = e >= 0
        at = jnp.where(live, count, -1)
        out = jnp.where(place == at, e - first, out)
        count = count + jnp.where(live, 1, 0)
    return out, count


def items(near, count, dead, out_ref, at):
    slots, targets = near.shape
    mine = (count + 1) // 2
    before = jnp.where(iota((targets, targets), 0) < iota((targets, targets), 1), 1.0, 0.0).astype(bf16)
    start = dot(jnp.broadcast_to(mine.astype(f32), (8, targets)).astype(bf16), before)[0:1]
    total = jnp.sum(mine, axis=1, keepdims=True).astype(f32)
    table = near.astype(f32).astype(bf16)
    rows = out_ref.shape[0] - at - 1
    wide = iota((rows, targets), 1)
    slot = iota((rows, slots), 1)
    lane = iota((rows, 128), 1)
    out = jnp.zeros((rows, 128), f32)
    for u in range(UNROLL):
        place = (iota((rows, 1), 0) * UNROLL + (u - LEAD)).astype(f32)
        begun = start <= place
        target = jnp.sum(jnp.where(begun, 1.0, 0.0), axis=1, keepdims=True) - 1.0
        base = jnp.max(jnp.where(begun, start, 0.0), axis=1, keepdims=True)
        pick = jnp.where(wide.astype(f32) == target, 1.0, 0.0).astype(bf16)
        lists = dot_t(pick, table)
        used = (place >= 0.0) & (place < total)
        first = 2.0 * (place - base)
        out = jnp.where(lane == u, jnp.where(used, target, float(targets)), out)
        for h in range(2):
            chosen = jnp.where(slot.astype(f32) == first + float(h), lists, 0.0)
            ids = jnp.where(used, jnp.sum(chosen, axis=1, keepdims=True), float(dead))
            out = jnp.where(lane == (h + 1) * UNROLL + u, ids, out)
    out_ref[at : at + rows] = out.astype(jnp.int32)
    out_ref[at + rows :] = jnp.broadcast_to(total, (1, 128)).astype(jnp.int32)


def list_rows(slots, leaves):
    return leaves + -(-(leaves * (slots // 2) // UNROLL + 3) // 8) * 8 + 1


def pack_kernel(target_ref, density_ref, out_ref, count_ref, slot_ref, *, peers, per):
    leaves, nrhs, leaf = density_ref.shape
    for d in range(peers):
        count_ref[d] = 0
    for k in range(leaves):
        t = target_ref[k]
        d = t // leaves
        c = count_ref[d]
        count_ref[d] = c + 1
        slot_ref[d * per + c] = t - d * leaves
        out_ref[d, pl.ds(pl.multiple_of(c * nrhs, nrhs), nrhs), :] = density_ref[k]
    row = iota((16, leaf), 0)
    for d in range(peers):
        x = jnp.zeros((16, leaf), f32)
        for c in range(per):
            x = jnp.where(row == c, slot_ref[d * per + c].astype(f32), x)
        out_ref[d, per * nrhs :, :] = x.astype(bf16)


def feature_kernel(
    node_list_ref, geo_ref, node_ref, near_ref, far_ref,
    fs_ref, fd_ref, ft_ref, wf_ref, split_ref, gn_ref, list_ref,
    pad_ref, npad_ref, fsn_ref, wfn_ref,
):
    leaves = fs_ref.shape[0]
    nodes_here = wfn_ref.shape[0]
    slots = near_ref.shape[0]
    index = lax.axis_index(AXES)
    first = index * leaves - REACH
    wide = leaves + 2 * REACH
    pad_ref[...] = jnp.zeros(pad_ref.shape, f32)
    pad_ref[0:6, :] = geo_ref[...]
    npad_ref[...] = jnp.zeros(npad_ref.shape, f32)
    npad_ref[0:3, :] = node_ref[...]
    near, near_count = compact(near_ref[...], first, wide)
    far, _ = compact(far_ref[...], first, wide)
    same = jnp.where(iota((leaves, leaves), 0) == iota((leaves, leaves), 1), 1.0, 0.0).astype(bf16)
    list_ref[0:leaves, 0:slots] = dot_t(same, far.astype(f32).astype(bf16)).astype(jnp.int32)
    items(near, near_count, wide, list_ref, leaves)

    def leaf_step(l, _):
        g = pad_ref[:, pl.ds(pl.multiple_of(l * 128, 128), 128)]
        f = Features(g)
        fs_ref[l], fd_ref[l] = sources(f)
        square = f.target_square()
        normal = f.target_normal()
        ft_ref[l] = jnp.concatenate(
            [
                jnp.concatenate(square + [f.zeros(64)], axis=0),
                jnp.concatenate([f.zeros(64)] + normal, axis=0),
            ],
            axis=1,
        ).astype(bf16)
        wf_ref[l] = pair_weights(square)[0]
        return 0

    lax.fori_loop(0, leaves, leaf_step, 0, unroll=4)

    def split_step(l, _):
        parts = []
        for k in range(2):
            parts += split3(pad_ref[:, pl.ds(pl.multiple_of((l * 2 + k) * 128, 128), 128)])
        split_ref[pl.ds(pl.multiple_of(l * 48, 48), 48), :] = jnp.concatenate(parts, axis=0).astype(bf16)
        return 0

    lax.fori_loop(0, leaves // 2, split_step, 0, unroll=4)

    def node_step(l, _):
        fsn_ref[l] = point_sources(Features(npad_ref[:, pl.ds(pl.multiple_of(l * 128, 128), 128)]))
        return 0

    n_nodes = 2 * fsn_ref.shape[0]
    lax.fori_loop(0, n_nodes // 2, node_step, 0, unroll=4)
    chunk = index * (nodes_here // 2)
    for l in range(nodes_here // 2):
        f = Features(npad_ref[:, pl.ds(pl.multiple_of((chunk + l) * 128, 128), 128)])
        wfn_ref[2 * l], wfn_ref[2 * l + 1] = pair_weights(f.target_square())

    node_slots = node_list_ref.shape[1]
    left = iota((64, 128), 1) < 64

    def node_field(p, _):
        x = []
        for j in range(0, node_slots, 2):
            pair = []
            for u in range(2):
                s = jnp.maximum(node_list_ref[p, j + u], 0)
                pair.append(fsn_ref[s // 2, pl.ds(pl.multiple_of((s % 2) * 64, 64), 64), :])
            x.append(jnp.where(left, pair[0], pair[1]))
        out = dot(jnp.concatenate(x, axis=0), wfn_ref[p])
        gn_ref[p] = (lax.rsqrt(out) * inv_four_pi).astype(bf16)
        return 0

    lax.fori_loop(0, nodes_here, node_field, 0)


def skeleton_kernel(
    arrived_ref, basis_ref, transfer_ref, split_ref, own_ref, a_ref, b_ref, node_ref, *, per
):
    peers = arrived_ref.shape[0]
    leaves = peers * per
    nrhs = 32
    half = leaves // 2
    for d in range(peers):
        slots = arrived_ref[d, per * nrhs :, :].astype(f32).astype(jnp.int32)
        for c in range(per):
            s = slots[c, 0]
            h = s // half
            own_ref[h, pl.ds(pl.multiple_of((s - h * half) * nrhs, nrhs), nrhs), :] = arrived_ref[
                d, c * nrhs : (c + 1) * nrhs, :
            ]
    left = iota((nrhs, 128), 1) < 64
    skels = []
    for p in range(leaves // 2):
        h, q = divmod(p, half // 2)
        out = dot_t(own_ref[h, q * 64 : (q + 1) * 64, :], basis_ref[p])
        pair = jnp.where(left, out[:nrhs], out[nrhs:]).astype(bf16)
        own_ref[h, half * nrhs + q * nrhs : half * nrhs + (q + 1) * nrhs, :] = pair
        skels.append(pair)
    base = half * nrhs + (half // 2) * nrhs
    n_split = half * 24
    for h in range(2):
        own_ref[h, base : base + n_split, :] = split_ref[h * n_split : (h + 1) * n_split, :]
    kids = transfer_ref.shape[2] // 128
    n_pairs = len(skels) // (2 * kids)
    for p in range(n_pairs):
        stack = jnp.concatenate(
            [jnp.concatenate(skels[(2 * p + h) * kids : (2 * p + h + 1) * kids], axis=1) for h in range(2)], axis=0
        )
        out = dot_t(stack, transfer_ref[p])
        pair = jnp.where(left, out[:nrhs], out[nrhs:]).astype(bf16)
        for d in range(peers):
            node_ref[d, p * nrhs : (p + 1) * nrhs, :] = pair
    odd = lax.axis_index(AXES) % 2
    a_ref[...] = own_ref[1 - odd]
    b_ref[...] = own_ref[odd]


def doubled(pairs, out_ref, k):
    rows = pairs.shape[0]
    i, j = iota((128, 256), 0), iota((128, 256), 1)
    pick = jnp.where(i == (j % 64) + 64 * (j // 128), 1.0, 0.0).astype(bf16)
    both = dot(pairs, pick).astype(bf16)
    for p in range(rows // 32):
        for h in range(2):
            out_ref[k + 2 * p + h] = both[32 * p : 32 * p + 32, 128 * h : 128 * h + 128]


def far_left(ids, skel_ref):
    left = iota((32, 128), 1) < 64
    cols = []
    for j in range(0, len(ids), 4):
        a, b, c, d = (skel_ref[s] for s in ids[j : j + 4])
        cols.append(jnp.concatenate([jnp.where(left, a, c), jnp.where(left, b, d)], axis=0))
    return jnp.concatenate(cols, axis=1)


def leaf_kernel(
    list_ref, fs_own_ref, fd_own_ref, ft_hbm, wf_hbm, own_ref, a_ref, b_ref,
    near_out, far_out,
    fs_ref, fd_ref, ft_ref, wf_ref, dens_ref, skel_ref, k_ref, g_ref, sem,
):
    leaves = wf_ref.shape[0]
    nrhs = 32
    half = leaves // 2
    wide = leaves + 2 * REACH
    odd = lax.axis_index(AXES) % 2 == 1
    slots = g_ref.shape[1] // 32
    mine = pl.ds(REACH, leaves)
    copies = [
        pltpu.make_async_copy(fs_own_ref, fs_ref.at[mine], sem.at[0]),
        pltpu.make_async_copy(ft_hbm, ft_ref.at[pl.ds(0, leaves)], sem.at[1]),
        pltpu.make_async_copy(fd_own_ref, fd_ref.at[mine], sem.at[2]),
        pltpu.make_async_copy(wf_hbm, wf_ref, sem.at[3]),
        pltpu.make_async_copy(fs_own_ref.at[0], fs_ref.at[wide], sem.at[4]),
        pltpu.make_async_copy(fd_own_ref.at[0], fd_ref.at[wide], sem.at[5]),
    ]
    for c in copies:
        c.start()

    base = half * nrhs + (half // 2) * nrhs
    for right, k in ((False, 0), (True, REACH + leaves)):

        def halo(l, _, right=right, k=k):
            at = pl.ds(pl.multiple_of(base + l * 48, 16), 48)
            x, y = a_ref[at, :].astype(f32), b_ref[at, :].astype(f32)
            x = jnp.where(odd, y, x) if right else jnp.where(odd, x, y)
            for j in range(2):
                g = x[24 * j : 24 * j + 8] + x[24 * j + 8 : 24 * j + 16] + x[24 * j + 16 : 24 * j + 24]
                fs_ref[k + 2 * l + j], fd_ref[k + 2 * l + j] = sources(Features(g))
            return 0

        lax.fori_loop(0, half // 2, halo, 0, unroll=2)

    def fill(view, k):
        for l in range(half):
            dens_ref[k + l] = view(l * nrhs, nrhs)
        doubled(view(half * nrhs, half // 2 * nrhs), skel_ref, k)

    fill(lambda at, n: jnp.where(odd, a_ref[at : at + n, :], b_ref[at : at + n, :]), 0)
    fill(lambda at, n: own_ref[0, at : at + n, :], REACH)
    fill(lambda at, n: own_ref[1, at : at + n, :], REACH + half)
    fill(lambda at, n: jnp.where(odd, b_ref[at : at + n, :], a_ref[at : at + n, :]), REACH + leaves)
    dens_ref[wide] = jnp.zeros((nrhs, 128), bf16)
    skel_ref[wide] = jnp.zeros((nrhs, 128), bf16)
    near_out[...] = jnp.zeros(near_out.shape, f32)
    for c in copies:
        c.wait()

    def item(i, u, part):
        return list_ref[leaves + i, part * UNROLL + u]

    def near_step(i, _):
        for u in range(UNROLL):
            lhs = jnp.concatenate([dens_ref[item(i, u, 1)], dens_ref[item(i, u, 2)]], axis=1)
            near_out[item(i, u, 0)] += dot(lhs, k_ref[u])
        for u in range(UNROLL):
            x = jnp.concatenate([fs_ref[item(i + 1, u, 1)], fs_ref[item(i + 1, u, 2)]], axis=0)
            out = dot(x, ft_ref[item(i + 1, u, 0)])
            r = lax.rsqrt(out[:, :128])
            k_ref[u] = ((out[:, 128:] * r) * (r * r)).astype(bf16)
        return 0

    n = list_ref[list_ref.shape[0] - 1, 0]
    lax.fori_loop(0, (n + UNROLL - 1) // UNROLL + 1, near_step, 0)

    left = iota((nrhs, 128), 1) < 64
    left64 = iota((64, 128), 1) < 64

    def far_ids(t):
        return [list_ref[t, u] for u in range(slots)]

    def far_step(p, _):
        done = jnp.maximum(p - 1, 0)
        e, o = (dot(far_left(far_ids(2 * done + h), skel_ref), g_ref[h]) for h in range(2))
        even = e[:nrhs] + pltpu.roll(e[nrhs:], 64, 1)
        odd_ = pltpu.roll(o[:nrhs], 64, 1) + o[nrhs:]
        far_out[done] = jnp.where(left, even, odd_)
        for h in range(2):
            t = 2 * jnp.minimum(p, half - 1) + h
            ids = far_ids(t)
            x = [
                jnp.where(left64, fd_ref[ids[j]], fd_ref[ids[j + 1]]) for j in range(0, slots, 2)
            ]
            out = dot(jnp.concatenate(x, axis=0), wf_ref[t])
            g_ref[h] = (lax.rsqrt(out) * inv_four_pi).astype(bf16)
        return 0

    lax.fori_loop(0, half + 1, far_step, 0)


def node_kernel(
    list_ref, near_ref, far_ref, skel_ref, gn_ref, transfer_ref, basis_ref,
    out_ref,
    all_ref,
):
    nrhs = 32
    nodes_here = gn_ref.shape[0]
    pairs = skel_ref.shape[0] // nrhs
    doubled(skel_ref[...], all_ref, 0)
    all_ref[2 * pairs] = jnp.zeros((nrhs, 128), bf16)
    slots = list_ref.shape[1]
    left = iota((nrhs, 128), 1) < 64
    kids = transfer_ref.shape[2] // 128

    def node(p, _):
        ids = []
        for j in range(slots):
            e = list_ref[p, j]
            ids.append(jnp.where(e < 0, 2 * pairs, e))
        acc = dot(far_left(ids, all_ref), gn_ref[p])
        x = acc[:nrhs] + pltpu.roll(acc[nrhs:], 64, 1)
        down = dot(x[:, :64].astype(bf16), transfer_ref[p])
        for c in range(kids):
            q = p * kids + c
            local = (far_ref[q] + down[:, c * 128 : (c + 1) * 128]).astype(bf16).astype(f32)
            both = jnp.concatenate(
                [jnp.where(left, local, 0.0), jnp.where(left, 0.0, local)], axis=0
            ).astype(bf16)
            y = dot(both, basis_ref[q])
            out_ref[2 * q] = (near_ref[2 * q] + y[:nrhs]).astype(bf16)
            out_ref[2 * q + 1] = (near_ref[2 * q + 1] + y[nrhs:]).astype(bf16)
        return 0

    lax.fori_loop(0, nodes_here, node, 0)


def vmem():
    return pl.BlockSpec(memory_space=pltpu.VMEM)


def smem():
    return pl.BlockSpec(memory_space=pltpu.SMEM)


def call(kernel, out, in_specs, scratch, name, flops, vmem_mib):
    many = isinstance(out, tuple)
    return pl.pallas_call(
        kernel,
        out_shape=out,
        in_specs=in_specs,
        out_specs=tuple(vmem() for _ in out) if many else vmem(),
        scratch_shapes=scratch,
        name=name,
        cost_estimate=pl.CostEstimate(flops=flops, bytes_accessed=1 << 20, transcendentals=0),
        compiler_params=pltpu.CompilerParams(vmem_limit_bytes=vmem_mib << 20),
    )


def pack(peers, per, density, leaf_target):
    leaves, nrhs, leaf = density.shape
    return call(
        lambda *r: pack_kernel(*r, peers=peers, per=per),
        jax.ShapeDtypeStruct((peers, per * nrhs + 16, leaf), bf16),
        [smem(), vmem()],
        [pltpu.SMEM((peers,), jnp.int32), pltpu.SMEM((leaves,), jnp.int32)],
        "pack",
        1 << 20,
        2,
    )(hbm(leaf_target), hbm(density))


def features(node_list, geometry, node_points, near_list, far_list):
    leaves, slots = near_list.shape
    nodes = node_points.shape[1] // 64
    nodes_here, node_slots = node_list.shape
    shape = jax.ShapeDtypeStruct
    return call(
        feature_kernel,
        (
            pltpu.HBM((leaves, 128, 128), bf16),
            pltpu.HBM((leaves, 64, 128), bf16),
            pltpu.HBM((leaves, 128, 256), bf16),
            pltpu.HBM((leaves, 128, 128), bf16),
            pltpu.VMEM((leaves * 24, 128), bf16),
            pltpu.VMEM((nodes_here, node_slots * 32, 128), bf16),
            pltpu.HBM((list_rows(slots, leaves), 128), jnp.int32),
        ),
        [smem()] + [vmem()] * 4,
        [
            pltpu.VMEM((8, leaves * 128), f32),
            pltpu.VMEM((8, nodes * 64), f32),
            pltpu.VMEM((nodes // 2, 128, 128), bf16),
            pltpu.VMEM((nodes_here, 128, 128), bf16),
        ],
        "features",
        1 << 30,
        14,
    )(hbm(node_list), hbm(geometry), hbm(node_points), hbm(near_list.T), hbm(far_list.T))


def skeletons(arrived, basis_in, transfer, split, per):
    peers = arrived.shape[0]
    leaves = peers * per
    nodes_here = transfer.shape[0]
    rows = leaves // 2 * 32 + leaves // 4 * 32 + leaves // 2 * 24
    shape = jax.ShapeDtypeStruct
    return call(
        lambda *r: skeleton_kernel(*r, per=per),
        (
            pltpu.VMEM((2, rows, 128), bf16),
            shape((rows, 128), bf16),
            shape((rows, 128), bf16),
            shape((peers, nodes_here // 2 * 32, 128), bf16),
        ),
        [vmem()] * 4,
        [],
        "skeleton",
        1 << 26,
        6,
    )(
        arrived,
        hbm(basis_in.reshape(leaves // 2, 128, -1)),
        hbm(transfer.reshape(nodes_here // 2, 128, -1)),
        split,
    )


def leaf_fields(slots, lists, fs, fd, ft, wf, own, got_a, got_b):
    leaves = ft.shape[0]
    wide = leaves + 2 * REACH
    anywhere = pl.BlockSpec(memory_space=pl.ANY)
    return call(
        leaf_kernel,
        (pltpu.VMEM((leaves + 1, 32, 128), f32), pltpu.VMEM((leaves // 2, 32, 128), f32)),
        [smem()] + [anywhere] * 4 + [vmem()] * 3,
        [
            pltpu.VMEM((wide + 1, 128, 128), bf16),
            pltpu.VMEM((wide + 1, 64, 128), bf16),
            pltpu.VMEM((leaves + 1, 128, 256), bf16),
            pltpu.VMEM((leaves, 128, 128), bf16),
            pltpu.VMEM((wide + 1, 32, 128), bf16),
            pltpu.VMEM((wide + 1, 32, 128), bf16),
            pltpu.VMEM((UNROLL, 256, 128), bf16),
            pltpu.VMEM((2, slots * 32, 128), bf16),
            pltpu.SemaphoreType.DMA((6,)),
        ],
        "leaves",
        1 << 31,
        20,
    )(hbm(lists), hbm(fs), hbm(fd), hbm(ft), hbm(wf), own, got_a, got_b)


def finish(node_list, near, far, all_skel, gn, transfer, basis_out):
    leaves, _, leaf = basis_out.shape
    nrhs = near.shape[1]
    nodes = all_skel.shape[0] // 16
    return call(
        node_kernel,
        jax.ShapeDtypeStruct((leaves, nrhs, leaf), bf16),
        [smem()] + [vmem()] * 6,
        [pltpu.VMEM((nodes + 1, nrhs, 128), bf16)],
        "nodes",
        1 << 28,
        8,
    )(hbm(node_list), near, far, all_skel, gn, hbm(transfer), hbm(basis_out.reshape(leaves // 2, 128, leaf)))


def hbm(x):
    return pltpu.with_memory_space_constraint(x, pltpu.HBM)


def on_device(
    density, leaf_target, geometry, near_list, far_list, node_list, basis_in, basis_out, transfer, node_points
):
    peers = lax.axis_size(AXES)
    per = density.shape[0] // peers
    outgoing = pack(peers, per, density, leaf_target)
    arrived = lax.all_to_all(outgoing, AXES, split_axis=0, concat_axis=0, tiled=True)
    fs, fd, ft, wf, split, gn, lists = features(node_list, geometry, node_points, near_list, far_list)
    own, to_a, to_b, node_out = skeletons(arrived, basis_in, transfer, split, per)
    all_skel = lax.all_to_all(node_out, AXES, split_axis=0, concat_axis=0, tiled=True)
    swap_a = [(i, i ^ 1) for i in range(peers)]
    swap_b = [(i, i + 1) for i in range(1, peers - 1, 2)] + [(i + 1, i) for i in range(1, peers - 1, 2)]
    got_a = lax.ppermute(to_a, AXES, swap_a)
    got_b = lax.ppermute(to_b, AXES, swap_b)
    near, far = leaf_fields(near_list.shape[1], lists, fs, fd, ft, wf, own, got_a, got_b)
    return finish(node_list, near, far, all_skel.reshape(-1, 128), gn, transfer, basis_out)


def solution(mesh):
    split = ("grp", "row", "col")
    return jax.shard_map(
        on_device,
        mesh=mesh,
        in_specs=(
            P(split, None, None),
            P(split),
            P(None, split),
            P(split, None),
            P(split, None),
            P(split, None),
            P(split, None, None),
            P(split, None, None),
            P(split, None, None),
            P(None, "grp"),
        ),
        out_specs=P(split, None, None),
        check_vma=False,
    )
```

profile of v0, /device:TPU:11, one launch (start us, length us, event | category | flops | bytes accessed | tf_op | source)
XLA Modules:
  0.0 60.3 jit_solution(9799578301747788276)
XLA Ops:
  0.0 2.0 %pack.1 = bf16[16,80,128]{2,1,0:T(8,128)(2,1)} custom-call(s32[32]{0:T(128)} %r_0_.1, bf16[32,32,128]{2,1,0:T(8,128)(2,1)} %r_1_.1), custom_call_target="tpu_custom_call" | custom-call | flops 1048576 | bytes 1048576 | tf_op jit(solution)/shard_map/pack/pallas_call | solution.py:522
  2.0 6.6 %all-to-all-start = ((bf16[16,80,128]{2,1,0:T(8,128)(2,1)}), bf16[16,80,128]{2,1,0:T(8,128)(2,1)S(1)}, u32[]{:S(2)}, u32[]{:S(2)}) async-start(bf16[16,80,128]{2,1,0:T(8,128)(2,1)} %pack.1), calls=%async_computation | async-start | bytes 655360 | tf_op jit(solution)/shard_map/all_to_all | solution.py:639
  8.6 7.6 %features.1 = (bf16[32,128,128]{2,1,0:T(8,128)(2,1)}, bf16[32,64,128]{2,1,0:T(8,128)(2,1)}, bf16[32,128,256]{2,1,0:T(8,128)(2,1)}, bf16[32,128,128]{2,1,0:T(8,12...) custom-call(s32[4,32]{1,0:T(4,128)} %list_ref.1, f32[6,4096]{1,0:T(8,128)} %geo_ref.1, ...), custom_call_target="tpu_custom_call" | custom-call | flops 1073741824 | bytes 1048576 | tf_op jit(solution)/shard_map/features/pallas_call | solution.py:538
  16.2 2.4 %all-to-all-done.r_0_ = bf16[16,80,128]{2,1,0:T(8,128)(2,1)S(1)} async-done(((bf16[16,80,128]{2,1,0:T(8,128)(2,1)}), bf16[16,80,128]{2,1,0:T(8,128)(2,1)S(1)}, u32[]{:S(2)}, u32[]{:S(2)}) %all-to-all-start) | async-done | bytes 327712 | tf_op jit(solution)/shard_map/all_to_all | solution.py:639
  18.7 2.6 %skeleton.1 = (bf16[2,1152,128]{2,1,0:T(8,128)(2,1)S(1)}, bf16[1152,128]{1,0:T(8,128)(2,1)S(1)}, bf16[1152,128]{1,0:T(8,128)(2,1)S(1)}, bf16[16,64,128]{2,1,0:T(8,128)(2,1)}) custom-call(bf16[16,80,128]{2,1,0:T(8,128)(2,1)S(1)} %all-to-all-done.r_0_, bf16[16,128,128]{2,1,0:T(8,128)(2,1)} %bitcast.8, bf16[2,128,512]{2,1,0:T(8,128)(2,1)} %bitcast.7, ...), custom_call_target="tpu_custom_call" | custom-call | flops 67108864 | bytes 1048576 | tf_op jit(solution)/shard_map/skeleton/pallas_call | solution.py:568
  21.3 0.0 collective-permute-start
  21.3 2.8 %collective-permute-start.1 = (bf16[1152,128]{1,0:T(8,128)(2,1)S(1)}, bf16[1152,128]{1,0:T(8,128)(2,1)S(1)}, u32[]{:S(2)}, u32[]{:S(2)}) collective-permute-start(bf16[1152,128]{1,0:T(8,128)(2,1)S(1)} %get-tuple-element.26), channel_id=1, source_target_pairs={{1,2},{3,4},{5,6},{7,8},{9,10},{11,12},{13,14},{2,1},{4,3},{6,5},{... | collective-permute-start | bytes 884744 | tf_op jit(solution)/shard_map/ppermute | solution.py:646
  24.1 4.5 %all-to-all-start.1 = ((bf16[16,64,128]{2,1,0:T(8,128)(2,1)}), bf16[16,64,128]{2,1,0:T(8,128)(2,1)S(1)}, u32[]{:S(2)}, u32[]{:S(2)}) async-start(bf16[16,64,128]{2,1,0:T(8,128)(2,1)} %get-tuple-element.29), calls=%async_computation.1 | async-start | bytes 524288 | tf_op jit(solution)/shard_map/all_to_all | solution.py:642
  28.6 0.0 collective-permute-done.a_ref
  28.6 5.1 %collective-permute-done.1.b_ref = bf16[1152,128]{1,0:T(8,128)(2,1)S(1)} collective-permute-done((bf16[1152,128]{1,0:T(8,128)(2,1)S(1)}, bf16[1152,128]{1,0:T(8,128)(2,1)S(1)}, u32[]{:S(2)}, u32[]{:S(2)}) %collective-permute-start.1) | collective-permute-done | bytes 294944 | tf_op jit(solution)/shard_map/ppermute | solution.py:646
  33.7 22.3 %leaves.1 = (f32[33,32,128]{2,1,0:T(8,128)S(1)}, f32[16,32,128]{2,1,0:T(8,128)S(1)}) custom-call(s32[73,128]{1,0:T(8,128)} %get-tuple-element.18.list_ref, bf16[32,128,128]{2,1,0:T(8,128)(2,1)} %get-tuple-element.19.fs_own_ref, bf16[32,64,128]{2,1,0:T(8,128)(2,1)} %get-tuple-element.20.fd_own_ref, bf16[32,128,256]{2,1,0:T(8,128)(2,1)} %get-tuple-element.21.ft_hbm, ...), custom_call_target="tpu_custom_call" | custom-call | flops 2147483648 | bytes 1048576 | tf_op jit(solution)/shard_map/leaves/pallas_call | solution.py:593
  56.0 0.0 all-to-all-done.1
  56.0 4.3 %nodes.1 = bf16[32,32,128]{2,1,0:T(8,128)(2,1)} custom-call(s32[4,32]{1,0:T(4,128)} %list_ref.1, f32[33,32,128]{2,1,0:T(8,128)S(1)} %get-tuple-element.27.near_ref, f32[16,32,128]{2,1,0:T(8,128)S(1)} %get-tuple-element.28.far_ref, bf16[1024,128]{1,0:T(8,128)(2,1)S(1)} %bitcast.6, bf16[4,1024,128]{2,1,0:T(8,128)(2,1)S(1)} %get-tuple-element.30.gn_ref, ...), custom_call_target="tpu_custom_call" | custom-call | flops 268435456 | bytes 1048576 | tf_op jit(solution)/shard_map/nodes/pallas_call | solution.py:618
Async XLA Ops:
  2.0 16.6 %all-to-all-start = ((bf16[16,80,128]{2,1,0:T(8,128)(2,1)}), bf16[16,80,128]{2,1,0:T(8,128)(2,1)S(1)}, u32[]{:S(2)}, u32[]{:S(2)}) async-start(bf16[16,80,128]{2,1,0:T(8,128)(2,1)} %pack.1), calls=%async_computation | async-start | bytes 655360 | tf_op jit(solution)/shard_map/all_to_all | solution.py:639
  21.3 7.3 %collective-permute-start = (bf16[1152,128]{1,0:T(8,128)(2,1)S(1)}, bf16[1152,128]{1,0:T(8,128)(2,1)S(1)}, u32[]{:S(2)}, u32[]{:S(2)}) collective-permute-start(bf16[1152,128]{1,0:T(8,128)(2,1)S(1)} %get-tuple-element.25), channel_id=1, source_target_pairs={{0,1},{1,0},{2,3},{3,2},{4,5},{5,4},{6,7},{7,6},{8,9},{9,8},{10,11... | collective-permute-start | bytes 884744 | tf_op jit(solution)/shard_map/ppermute | solution.py:645
  21.3 12.4 %collective-permute-start.1 = (bf16[1152,128]{1,0:T(8,128)(2,1)S(1)}, bf16[1152,128]{1,0:T(8,128)(2,1)S(1)}, u32[]{:S(2)}, u32[]{:S(2)}) collective-permute-start(bf16[1152,128]{1,0:T(8,128)(2,1)S(1)} %get-tuple-element.26), channel_id=1, source_target_pairs={{1,2},{3,4},{5,6},{7,8},{9,10},{11,12},{13,14},{2,1},{4,3},{6,5},{... | collective-permute-start | bytes 884744 | tf_op jit(solution)/shard_map/ppermute | solution.py:646
  24.1 31.9 %all-to-all-start.1 = ((bf16[16,64,128]{2,1,0:T(8,128)(2,1)}), bf16[16,64,128]{2,1,0:T(8,128)(2,1)S(1)}, u32[]{:S(2)}, u32[]{:S(2)}) async-start(bf16[16,64,128]{2,1,0:T(8,128)(2,1)} %get-tuple-element.29), calls=%async_computation.1 | async-start | bytes 524288 | tf_op jit(solution)/shard_map/all_to_all | solution.py:642
where the time goes:
time: 60.4 us; the launch traced here: 60.3 us
  Pallas kernels  38.9 us (64%)
  starting transfers between devices  13.9 us (23%)
  waiting for transfers between devices  7.53 us (12%)
    pallas_call x1, Pallas kernels, leaf_fields(): call(leaf_kernel, (pltpu.VMEM((leaves + 1, 32, 128), f32), pltpu.VMEM((le...  22.3 us
    pallas_call x1, Pallas kernels, features(): call(feature_kernel, (pltpu.HBM((leaves, 128, 128), bf16), pltpu.HBM((lea...  7.63 us
    all_to_all x1, starting transfers between devices, on_device(): lax.all_to_all(outgoing, AXES, split_axis=0, concat_axis=0, tiled=True)  6.58 us
    ppermute x1, waiting for transfers between devices, on_device(): got_b = lax.ppermute(to_b, AXES, swap_b)  5.12 us
    all_to_all x1, starting transfers between devices, on_device(): lax.all_to_all(node_out, AXES, split_axis=0, concat_axis=0, tiled=True)  4.52 us
    pallas_call x1, Pallas kernels, finish(): call(node_kernel, jax.ShapeDtypeStruct((leaves, nrhs, leaf), bf16), [smem...  4.27 us
    ppermute x1, starting transfers between devices, on_device(): got_b = lax.ppermute(to_b, AXES, swap_b)  2.79 us
    pallas_call x1, Pallas kernels, skeletons(): call(lambda *r: skeleton_kernel(*r, per=per), (pltpu.VMEM((2, rows, 128),...  2.64 us
  transfers between devices with their start and end apart: 4, of which 2 were waited for; matrix products, arithmetic and copies ran while one was open for 0% of the time, Pallas kernels for 50%

commit v1 on v0

--- a/solution.py
+++ b/solution.py
@@ -174,14 +174,14 @@
     return out, count
 
 
-def items(near, count, dead, out_ref, at):
+def items(near, count, dead, out_ref):
     slots, targets = near.shape
     mine = (count + 1) // 2
     before = jnp.where(iota((targets, targets), 0) < iota((targets, targets), 1), 1.0, 0.0).astype(bf16)
     start = dot(jnp.broadcast_to(mine.astype(f32), (8, targets)).astype(bf16), before)[0:1]
     total = jnp.sum(mine, axis=1, keepdims=True).astype(f32)
     table = near.astype(f32).astype(bf16)
-    rows = out_ref.shape[0] - at - 1
+    rows = out_ref.shape[0] - 1
     wide = iota((rows, targets), 1)
     slot = iota((rows, slots), 1)
     lane = iota((rows, 128), 1)
@@ -200,12 +200,12 @@
             chosen = jnp.where(slot.astype(f32) == first + float(h), lists, 0.0)
             ids = jnp.where(used, jnp.sum(chosen, axis=1, keepdims=True), float(dead))
             out = jnp.where(lane == (h + 1) * UNROLL + u, ids, out)
-    out_ref[at : at + rows] = out.astype(jnp.int32)
-    out_ref[at + rows :] = jnp.broadcast_to(total, (1, 128)).astype(jnp.int32)
+    out_ref[0:rows] = out.astype(jnp.int32)
+    out_ref[rows:] = jnp.broadcast_to(total, (1, 128)).astype(jnp.int32)
 
 
 def list_rows(slots, leaves):
-    return leaves + -(-(leaves * (slots // 2) // UNROLL + 3) // 8) * 8 + 1
+    return -(-(leaves * (slots // 2) // UNROLL + 3) // 8) * 8 + 1
 
 
 def pack_kernel(target_ref, density_ref, out_ref, count_ref, slot_ref, *, peers, per):
@@ -219,9 +219,9 @@
         count_ref[d] = c + 1
         slot_ref[d * per + c] = t - d * leaves
         out_ref[d, pl.ds(pl.multiple_of(c * nrhs, nrhs), nrhs), :] = density_ref[k]
-    row = iota((16, leaf), 0)
+    row = iota((8, leaf), 0)
     for d in range(peers):
-        x = jnp.zeros((16, leaf), f32)
+        x = jnp.zeros((8, leaf), f32)
         for c in range(per):
             x = jnp.where(row == c, slot_ref[d * per + c].astype(f32), x)
         out_ref[d, per * nrhs :, :] = x.astype(bf16)
@@ -229,7 +229,7 @@
 
 def feature_kernel(
     node_list_ref, geo_ref, node_ref, near_ref, far_ref,
-    fs_ref, fd_ref, ft_ref, wf_ref, split_ref, gn_ref, list_ref,
+    fs_ref, fd_ref, ft_ref, wf_ref, split_ref, gn_ref, own_list_ref, halo_list_ref, far_list_ref,
     pad_ref, npad_ref, fsn_ref, wfn_ref,
 ):
     leaves = fs_ref.shape[0]
@@ -242,11 +242,13 @@
     pad_ref[0:6, :] = geo_ref[...]
     npad_ref[...] = jnp.zeros(npad_ref.shape, f32)
     npad_ref[0:3, :] = node_ref[...]
-    near, near_count = compact(near_ref[...], first, wide)
+    entries = near_ref[...]
+    local = (entries >= index * leaves) & (entries < (index + 1) * leaves)
+    items(*compact(jnp.where(local, entries, -1), index * leaves, leaves), leaves, own_list_ref)
+    items(*compact(jnp.where(local, -1, entries), first, wide), wide, halo_list_ref)
     far, _ = compact(far_ref[...], first, wide)
     same = jnp.where(iota((leaves, leaves), 0) == iota((leaves, leaves), 1), 1.0, 0.0).astype(bf16)
-    list_ref[0:leaves, 0:slots] = dot_t(same, far.astype(f32).astype(bf16)).astype(jnp.int32)
-    items(near, near_count, wide, list_ref, leaves)
+    far_list_ref[:, 0:slots] = dot_t(same, far.astype(f32).astype(bf16)).astype(jnp.int32)
 
     def leaf_step(l, _):
         g = pad_ref[:, pl.ds(pl.multiple_of(l * 128, 128), 128)]
@@ -365,9 +367,49 @@
     return jnp.concatenate(cols, axis=1)
 
 
+def near_pairs(list_ref, fs_ref, ft_ref, dens_ref, k_ref, near_ref):
+    def item(i, u, part):
+        return list_ref[i, part * UNROLL + u]
+
+    def step(i, _):
+        for u in range(UNROLL):
+            lhs = jnp.concatenate([dens_ref[item(i, u, 1)], dens_ref[item(i, u, 2)]], axis=1)
+            near_ref[item(i, u, 0)] += dot(lhs, k_ref[u])
+        for u in range(UNROLL):
+            x = jnp.concatenate([fs_ref[item(i + 1, u, 1)], fs_ref[item(i + 1, u, 2)]], axis=0)
+            out = dot(x, ft_ref[item(i + 1, u, 0)])
+            r = lax.rsqrt(out[:, :128])
+            k_ref[u] = ((out[:, 128:] * r) * (r * r)).astype(bf16)
+        return 0
+
+    n = list_ref[list_ref.shape[0] - 1, 0]
+    lax.fori_loop(0, (n + UNROLL - 1) // UNROLL + 1, step, 0)
+
+
+def own_kernel(list_ref, fs_hbm, ft_hbm, own_ref, near_ref, fs_ref, ft_ref, dens_ref, k_ref, sem):
+    leaves = fs_hbm.shape[0]
+    half = leaves // 2
+    nrhs = 32
+    copies = [
+        pltpu.make_async_copy(fs_hbm, fs_ref.at[pl.ds(0, leaves)], sem.at[0]),
+        pltpu.make_async_copy(ft_hbm, ft_ref.at[pl.ds(0, leaves)], sem.at[1]),
+        pltpu.make_async_copy(fs_hbm.at[0], fs_ref.at[leaves], sem.at[2]),
+    ]
+    for c in copies:
+        c.start()
+    for l in range(leaves):
+        dens_ref[l] = own_ref[l // half, l % half * nrhs : (l % half + 1) * nrhs, :]
+    dens_ref[leaves] = jnp.zeros((nrhs, 128), bf16)
+    near_ref[...] = jnp.zeros(near_ref.shape, f32)
+    for c in copies:
+        c.wait()
+    near_pairs(list_ref, fs_ref, ft_ref, dens_ref, k_ref, near_ref)
+
+
 def leaf_kernel(
-    list_ref, fs_own_ref, fd_own_ref, ft_hbm, wf_hbm, own_ref, a_ref, b_ref,
-    near_out, far_out,
+    list_ref, far_list_ref, fs_own_ref, fd_own_ref, ft_hbm, wf_hbm, own_ref, a_ref, b_ref, first_ref,
+    basis_hbm, transfer_hbm,
+    near_out, far_out, basis_out_ref, transfer_out_ref,
     fs_ref, fd_ref, ft_ref, wf_ref, dens_ref, skel_ref, k_ref, g_ref, sem,
 ):
     leaves = wf_ref.shape[0]
@@ -378,14 +420,17 @@
     slots = g_ref.shape[1] // 32
     mine = pl.ds(REACH, leaves)
     copies = [
-        pltpu.make_async_copy(fs_own_ref, fs_ref.at[mine], sem.at[0]),
+        pltpu.make_async_copy(fd_own_ref, fd_ref.at[mine], sem.at[0]),
         pltpu.make_async_copy(ft_hbm, ft_ref.at[pl.ds(0, leaves)], sem.at[1]),
-        pltpu.make_async_copy(fd_own_ref, fd_ref.at[mine], sem.at[2]),
-        pltpu.make_async_copy(wf_hbm, wf_ref, sem.at[3]),
-        pltpu.make_async_copy(fs_own_ref.at[0], fs_ref.at[wide], sem.at[4]),
-        pltpu.make_async_copy(fd_own_ref.at[0], fd_ref.at[wide], sem.at[5]),
+        pltpu.make_async_copy(wf_hbm, wf_ref, sem.at[2]),
+        pltpu.make_async_copy(fs_own_ref.at[0], fs_ref.at[wide], sem.at[3]),
+        pltpu.make_async_copy(fd_own_ref.at[0], fd_ref.at[wide], sem.at[4]),
     ]
-    for c in copies:
+    ahead = [
+        pltpu.make_async_copy(basis_hbm, basis_out_ref, sem.at[5]),
+        pltpu.make_async_copy(transfer_hbm, transfer_out_ref, sem.at[6]),
+    ]
+    for c in copies + ahead:
         c.start()
 
     base = half * nrhs + (half // 2) * nrhs
@@ -402,43 +447,28 @@
 
         lax.fori_loop(0, half // 2, halo, 0, unroll=2)
 
-    def fill(view, k):
-        for l in range(half):
-            dens_ref[k + l] = view(l * nrhs, nrhs)
+    def fill(view, k, dens=True):
+        if dens:
+            for l in range(half):
+                dens_ref[k + l] = view(l * nrhs, nrhs)
         doubled(view(half * nrhs, half // 2 * nrhs), skel_ref, k)
 
     fill(lambda at, n: jnp.where(odd, a_ref[at : at + n, :], b_ref[at : at + n, :]), 0)
-    fill(lambda at, n: own_ref[0, at : at + n, :], REACH)
-    fill(lambda at, n: own_ref[1, at : at + n, :], REACH + half)
+    fill(lambda at, n: own_ref[0, at : at + n, :], REACH, False)
+    fill(lambda at, n: own_ref[1, at : at + n, :], REACH + half, False)
     fill(lambda at, n: jnp.where(odd, b_ref[at : at + n, :], a_ref[at : at + n, :]), REACH + leaves)
     dens_ref[wide] = jnp.zeros((nrhs, 128), bf16)
     skel_ref[wide] = jnp.zeros((nrhs, 128), bf16)
-    near_out[...] = jnp.zeros(near_out.shape, f32)
+    near_out[...] = first_ref[...]
     for c in copies:
         c.wait()
-
-    def item(i, u, part):
-        return list_ref[leaves + i, part * UNROLL + u]
-
-    def near_step(i, _):
-        for u in range(UNROLL):
-            lhs = jnp.concatenate([dens_ref[item(i, u, 1)], dens_ref[item(i, u, 2)]], axis=1)
-            near_out[item(i, u, 0)] += dot(lhs, k_ref[u])
-        for u in range(UNROLL):
-            x = jnp.concatenate([fs_ref[item(i + 1, u, 1)], fs_ref[item(i + 1, u, 2)]], axis=0)
-            out = dot(x, ft_ref[item(i + 1, u, 0)])
-            r = lax.rsqrt(out[:, :128])
-            k_ref[u] = ((out[:, 128:] * r) * (r * r)).astype(bf16)
-        return 0
-
-    n = list_ref[list_ref.shape[0] - 1, 0]
-    lax.fori_loop(0, (n + UNROLL - 1) // UNROLL + 1, near_step, 0)
+    near_pairs(list_ref, fs_ref, ft_ref, dens_ref, k_ref, near_out)
 
     left = iota((nrhs, 128), 1) < 64
     left64 = iota((64, 128), 1) < 64
 
     def far_ids(t):
-        return [list_ref[t, u] for u in range(slots)]
+        return [far_list_ref[t, u] for u in range(slots)]
 
     def far_step(p, _):
         done = jnp.maximum(p - 1, 0)
@@ -457,6 +487,8 @@
         return 0
 
     lax.fori_loop(0, half + 1, far_step, 0)
+    for c in ahead:
+        c.wait()
 
 
 def node_kernel(
@@ -521,7 +553,7 @@
     leaves, nrhs, leaf = density.shape
     return call(
         lambda *r: pack_kernel(*r, peers=peers, per=per),
-        jax.ShapeDtypeStruct((peers, per * nrhs + 16, leaf), bf16),
+        jax.ShapeDtypeStruct((peers, per * nrhs + 8, leaf), bf16),
         [smem(), vmem()],
         [pltpu.SMEM((peers,), jnp.int32), pltpu.SMEM((leaves,), jnp.int32)],
         "pack",
@@ -545,6 +577,8 @@
             pltpu.VMEM((leaves * 24, 128), bf16),
             pltpu.VMEM((nodes_here, node_slots * 32, 128), bf16),
             pltpu.HBM((list_rows(slots, leaves), 128), jnp.int32),
+            pltpu.HBM((list_rows(slots, leaves), 128), jnp.int32),
+            pltpu.HBM((leaves, 128), jnp.int32),
         ),
         [smem()] + [vmem()] * 4,
         [
@@ -580,20 +614,45 @@
         6,
     )(
         arrived,
-        hbm(basis_in.reshape(leaves // 2, 128, -1)),
-        hbm(transfer.reshape(nodes_here // 2, 128, -1)),
+        basis_in.reshape(leaves // 2, 128, -1),
+        transfer.reshape(nodes_here // 2, 128, -1),
         split,
     )
 
 
-def leaf_fields(slots, lists, fs, fd, ft, wf, own, got_a, got_b):
+def own_fields(own_list, fs, ft, own):
+    leaves = ft.shape[0]
+    anywhere = pl.BlockSpec(memory_space=pl.ANY)
+    return call(
+        own_kernel,
+        pltpu.VMEM((leaves + 1, 32, 128), f32),
+        [smem(), anywhere, anywhere, vmem()],
+        [
+            pltpu.VMEM((leaves + 1, 128, 128), bf16),
+            pltpu.VMEM((leaves + 1, 128, 256), bf16),
+            pltpu.VMEM((leaves + 1, 32, 128), bf16),
+            pltpu.VMEM((UNROLL, 256, 128), bf16),
+            pltpu.SemaphoreType.DMA((3,)),
+        ],
+        "own",
+        1 << 31,
+        12,
+    )(hbm(own_list), hbm(fs), hbm(ft), own)
+
+
+def leaf_fields(slots, halo_list, far_list, fs, fd, ft, wf, own, got_a, got_b, first, basis_out, transfer):
     leaves = ft.shape[0]
     wide = leaves + 2 * REACH
     anywhere = pl.BlockSpec(memory_space=pl.ANY)
     return call(
         leaf_kernel,
-        (pltpu.VMEM((leaves + 1, 32, 128), f32), pltpu.VMEM((leaves // 2, 32, 128), f32)),
-        [smem()] + [anywhere] * 4 + [vmem()] * 3,
+        (
+            pltpu.VMEM((leaves + 1, 32, 128), f32),
+            pltpu.VMEM((leaves // 2, 32, 128), f32),
+            pltpu.VMEM(basis_out.shape, bf16),
+            pltpu.VMEM(transfer.shape, bf16),
+        ),
+        [smem()] * 2 + [anywhere] * 4 + [vmem()] * 4 + [anywhere] * 2,
         [
             pltpu.VMEM((wide + 1, 128, 128), bf16),
             pltpu.VMEM((wide + 1, 64, 128), bf16),
@@ -603,16 +662,19 @@
             pltpu.VMEM((wide + 1, 32, 128), bf16),
             pltpu.VMEM((UNROLL, 256, 128), bf16),
             pltpu.VMEM((2, slots * 32, 128), bf16),
-            pltpu.SemaphoreType.DMA((6,)),
+            pltpu.SemaphoreType.DMA((7,)),
         ],
         "leaves",
         1 << 31,
         20,
-    )(hbm(lists), hbm(fs), hbm(fd), hbm(ft), hbm(wf), own, got_a, got_b)
+    )(
+        hbm(halo_list), hbm(far_list), hbm(fs), hbm(fd), hbm(ft), hbm(wf), own, hbm(got_a), hbm(got_b), first,
+        hbm(basis_out), hbm(transfer),
+    )
 
 
 def finish(node_list, near, far, all_skel, gn, transfer, basis_out):
-    leaves, _, leaf = basis_out.shape
+    leaves, leaf = 2 * basis_out.shape[0], basis_out.shape[2]
     nrhs = near.shape[1]
     nodes = all_skel.shape[0] // 16
     return call(
@@ -623,7 +685,7 @@
         "nodes",
         1 << 28,
         8,
-    )(hbm(node_list), near, far, all_skel, gn, hbm(transfer), hbm(basis_out.reshape(leaves // 2, 128, leaf)))
+    )(hbm(node_list), near, far, all_skel, gn, transfer, basis_out)
 
 
 def hbm(x):
@@ -637,14 +699,18 @@
     per = density.shape[0] // peers
     outgoing = pack(peers, per, density, leaf_target)
     arrived = lax.all_to_all(outgoing, AXES, split_axis=0, concat_axis=0, tiled=True)
-    fs, fd, ft, wf, split, gn, lists = features(node_list, geometry, node_points, near_list, far_list)
+    fs, fd, ft, wf, split, gn, own_pairs, halo_pairs, far_rows = features(node_list, geometry, node_points, near_list, far_list)
     own, to_a, to_b, node_out = skeletons(arrived, basis_in, transfer, split, per)
     all_skel = lax.all_to_all(node_out, AXES, split_axis=0, concat_axis=0, tiled=True)
     swap_a = [(i, i ^ 1) for i in range(peers)]
     swap_b = [(i, i + 1) for i in range(1, peers - 1, 2)] + [(i + 1, i) for i in range(1, peers - 1, 2)]
     got_a = lax.ppermute(to_a, AXES, swap_a)
     got_b = lax.ppermute(to_b, AXES, swap_b)
-    near, far = leaf_fields(near_list.shape[1], lists, fs, fd, ft, wf, own, got_a, got_b)
+    first = own_fields(own_pairs, fs, ft, own)
+    near, far, basis_out, transfer = leaf_fields(
+        near_list.shape[1], halo_pairs, far_rows, fs, fd, ft, wf, own, got_a, got_b, first,
+        basis_out.reshape(basis_out.shape[0] // 2, 128, -1), transfer,
+    )
     return finish(node_list, near, far, all_skel.reshape(-1, 128), gn, transfer, basis_out)
 
 

time: 60.4 us -> 57.5 us (0.952)
  the two profiles are of different devices: /device:TPU:11 before, /device:TPU:1 now
where the time goes in v1:
time: 57.5 us; the launch traced here: 56.9 us
  Pallas kernels  40.1 us (70%)
  starting transfers between devices  14 us (24%)
  waiting for transfers between devices  1.99 us (3%)
  local copies, waits for them, and re-layouts  0.8 us (1%)
    pallas_call x1, Pallas kernels, leaf_fields(): call(leaf_kernel, (pltpu.VMEM((leaves + 1, 32, 128), f32), pltpu.VMEM((le...  12.3 us
    pallas_call x1, Pallas kernels, own_fields(): call(own_kernel, pltpu.VMEM((leaves + 1, 32, 128), f32), [smem(), anywher...  12.2 us
    pallas_call x1, Pallas kernels, features(): call(feature_kernel, (pltpu.HBM((leaves, 128, 128), bf16), pltpu.HBM((lea...  8.23 us
    all_to_all x1, starting transfers between devices, on_device(): lax.all_to_all(outgoing, AXES, split_axis=0, concat_axis=0, tiled=True)  7.34 us
    all_to_all x1, starting transfers between devices, on_device(): lax.all_to_all(node_out, AXES, split_axis=0, concat_axis=0, tiled=True)  4.07 us
    pallas_call x1, Pallas kernels, finish(): call(node_kernel, jax.ShapeDtypeStruct((leaves, nrhs, leaf), bf16), [smem...  3.82 us
    ppermute x1, starting transfers between devices, on_device(): got_b = lax.ppermute(to_b, AXES, swap_b)  2.16 us
    pallas_call x1, Pallas kernels, pack(): call(lambda *r: pack_kernel(*r, peers=peers, per=per), jax.ShapeDtypeStru...  2.02 us
  transfers between devices with their start and end apart: 4, of which 1 were waited for; matrix products, arithmetic and copies ran while one was open for 0% of the time, Pallas kernels for 57%

profile of v1, /device:TPU:1, one launch (start us, length us, event | category | flops | bytes accessed | tf_op | source)
XLA Modules:
  0.0 56.9 jit_solution(9948218555193305694)
XLA Ops:
  0.0 2.0 %pack.1 = bf16[16,72,128]{2,1,0:T(8,128)(2,1)} custom-call(s32[32]{0:T(128)} %r_0_.1, bf16[32,32,128]{2,1,0:T(8,128)(2,1)} %r_1_.1), custom_call_target="tpu_custom_call" | custom-call | flops 1048576 | bytes 1048576 | tf_op jit(solution)/shard_map/pack/pallas_call | solution.py:554
  2.0 7.3 %all-to-all-start = ((bf16[16,72,128]{2,1,0:T(8,128)(2,1)}), bf16[16,72,128]{2,1,0:T(8,128)(2,1)S(1)}, u32[]{:S(2)}, u32[]{:S(2)}) async-start(bf16[16,72,128]{2,1,0:T(8,128)(2,1)} %pack.1), calls=%async_computation | async-start | bytes 589824 | tf_op jit(solution)/shard_map/all_to_all | solution.py:701
  9.4 0.0 copy-start
  9.4 0.0 copy-start.1
  9.4 8.2 %features.1 = (bf16[32,128,128]{2,1,0:T(8,128)(2,1)}, bf16[32,64,128]{2,1,0:T(8,128)(2,1)}, bf16[32,128,256]{2,1,0:T(8,128)(2,1)}, bf16[32,128,128]{2,1,0:T(8,12...) custom-call(s32[4,32]{1,0:T(4,128)} %list_ref.1, ...), custom_call_target="tpu_custom_call" | custom-call | flops 1073741824 | bytes 1048576 | tf_op jit(solution)/shard_map/features/pallas_call | solution.py:570
  17.6 2.0 %all-to-all-done.r_0_ = bf16[16,72,128]{2,1,0:T(8,128)(2,1)S(1)} async-done(((bf16[16,72,128]{2,1,0:T(8,128)(2,1)}), bf16[16,72,128]{2,1,0:T(8,128)(2,1)S(1)}, u32[]{:S(2)}, u32[]{:S(2)}) %all-to-all-start) | async-done | bytes 294944 | tf_op jit(solution)/shard_map/all_to_all | solution.py:701
  19.6 0.0 copy-done
  19.6 0.0 copy-done.1
  19.6 1.5 %skeleton.1 = (bf16[2,1152,128]{2,1,0:T(8,128)(2,1)S(1)}, bf16[1152,128]{1,0:T(8,128)(2,1)}, bf16[1152,128]{1,0:T(8,128)(2,1)S(1)}, bf16[16,64,128]{2,1,0:T(8,128)(2,1)}) custom-call(bf16[16,72,128]{2,1,0:T(8,128)(2,1)S(1)} %all-to-all-done.r_0_, bf16[16,128,128]{2,1,0:T(8,128)(2,1)S(1)} %bitcast.7, bf16[2,128,512]{2,1,0:T(8,128)(2,1)S(1)} %bitcast.8, ...), custom_call_target="tpu_custom_call" | custom-call | flops 67108864 | bytes 1048576 | tf_op jit(solution)/shard_map/skeleton/pallas_call | solution.py:602
  21.1 0.4 collective-permute-start
  21.5 2.2 %collective-permute-start.1 = (bf16[1152,128]{1,0:T(8,128)(2,1)S(1)}, bf16[1152,128]{1,0:T(8,128)(2,1)S(1)}, u32[]{:S(2)}, u32[]{:S(2)}) collective-permute-start(bf16[1152,128]{1,0:T(8,128)(2,1)S(1)} %get-tuple-element.31), channel_id=1, source_target_pairs={{1,2},{3,4},{5,6},{7,8},{9,10},{11,12},{13,14},{2,1},{4,3},{6,5},{... | collective-permute-start | bytes 884744 | tf_op jit(solution)/shard_map/ppermute | solution.py:708
  23.7 4.1 %all-to-all-start.1 = ((bf16[16,64,128]{2,1,0:T(8,128)(2,1)}), bf16[16,64,128]{2,1,0:T(8,128)(2,1)S(1)}, u32[]{:S(2)}, u32[]{:S(2)}) async-start(bf16[16,64,128]{2,1,0:T(8,128)(2,1)} %get-tuple-element.35), calls=%async_computation.1 | async-start | bytes 524288 | tf_op jit(solution)/shard_map/all_to_all | solution.py:704
  27.8 12.2 %own.1.first_ref = f32[33,32,128]{2,1,0:T(8,128)S(1)} custom-call(s32[41,128]{1,0:T(8,128)} %get-tuple-element.32.list_ref, bf16[32,128,128]{2,1,0:T(8,128)(2,1)} %get-tuple-element.24.fs_hbm.fs_own_ref, bf16[32,128,256]{2,1,0:T(8,128)(2,1)} %get-tuple-element.26.ft_hbm, bf16[2,1152,128]{2,1,0:T(8,128)(2,1)S(1)} %get-tuple-element.29.own_ref), custom_call_target="tpu_custom_call" | custom-call | flops 2147483648 | bytes 1048576 | tf_op jit(solution)/shard_map/own/pallas_call | solution.py:626
  40.0 0.0 collective-permute-done.a_ref
  40.0 0.0 copy-start.2
  40.0 0.0 collective-permute-done.1.b_ref
  40.0 0.0 copy-start.3
  40.0 0.7 %copy-done.2 = bf16[1152,128]{1,0:T(8,128)(2,1)} copy-done((bf16[1152,128]{1,0:T(8,128)(2,1)}, bf16[1152,128]{1,0:T(8,128)(2,1)S(1)}, u32[]{:S(2)}) %copy-start.2) | copy-done | bytes 294936
  40.8 0.1 copy-done.3
  40.8 12.3 %leaves.1 = (f32[33,32,128]{2,1,0:T(8,128)S(1)}, f32[16,32,128]{2,1,0:T(8,128)S(1)}, bf16[16,128,128]{2,1,0:T(8,128)(2,1)S(1)}, bf16[4,64,512]{2,1,0:T(8,128)(2,1)S(1)}) custom-call(s32[41,128]{1,0:T(8,128)} %get-tuple-element.22.list_ref, s32[32,128]{1,0:T(8,128)} %get-tuple-element.23.far_list_ref, ...), custom_call_target="tpu_custom_call" | custom-call | flops 2147483648 | bytes 1048576 | tf_op jit(solution)/shard_map/leaves/pallas_call | solution.py:647
  53.1 0.0 all-to-all-done.1
  53.1 3.8 %nodes.1 = bf16[32,32,128]{2,1,0:T(8,128)(2,1)} custom-call(s32[4,32]{1,0:T(4,128)} %list_ref.1, f32[33,32,128]{2,1,0:T(8,128)S(1)} %get-tuple-element.33.near_ref, f32[16,32,128]{2,1,0:T(8,128)S(1)} %get-tuple-element.34.far_ref, bf16[1024,128]{1,0:T(8,128)(2,1)S(1)} %bitcast.6, bf16[4,1024,128]{2,1,0:T(8,128)(2,1)S(1)} %get-tuple-element.36.gn_ref, ...), custom_call_target="tpu_custom_call" | custom-call | flops 268435456 | bytes 1048576 | tf_op jit(solution)/shard_map/nodes/pallas_call | solution.py:680
Async XLA Ops:
  2.0 17.6 %all-to-all-start = ((bf16[16,72,128]{2,1,0:T(8,128)(2,1)}), bf16[16,72,128]{2,1,0:T(8,128)(2,1)S(1)}, u32[]{:S(2)}, u32[]{:S(2)}) async-start(bf16[16,72,128]{2,1,0:T(8,128)(2,1)} %pack.1), calls=%async_computation | async-start | bytes 589824 | tf_op jit(solution)/shard_map/all_to_all | solution.py:701
  9.4 10.2 %copy-start = (bf16[32,64,128]{2,1,0:T(8,128)(2,1)S(1)}, bf16[32,64,128]{2,1,0:T(8,128)(2,1)}, u32[]{:S(2)}) copy-start(bf16[32,64,128]{2,1,0:T(8,128)(2,1)} %param.16) | copy-start | bytes 1572868
  9.4 10.2 %copy-start.1 = (bf16[4,64,512]{2,1,0:T(8,128)(2,1)S(1)}, bf16[4,64,512]{2,1,0:T(8,128)(2,1)}, u32[]{:S(2)}) copy-start(bf16[4,64,512]{2,1,0:T(8,128)(2,1)} %transfer_hbm.1) | copy-start | bytes 786436
  21.1 18.9 %collective-permute-start = (bf16[1152,128]{1,0:T(8,128)(2,1)}, bf16[1152,128]{1,0:T(8,128)(2,1)S(1)}, u32[]{:S(2)}, u32[]{:S(2)}) collective-permute-start(bf16[1152,128]{1,0:T(8,128)(2,1)} %get-tuple-element.30), channel_id=1, source_target_pairs={{0,1},{1,0},{2,3},{3,2},{4,5},{5,4},{6,7},{7,6},{8,9},{9,8},{10,11... | collective-permute-start | bytes 884744 | tf_op jit(solution)/shard_map/ppermute | solution.py:707
  21.5 18.5 %collective-permute-start.1 = (bf16[1152,128]{1,0:T(8,128)(2,1)S(1)}, bf16[1152,128]{1,0:T(8,128)(2,1)S(1)}, u32[]{:S(2)}, u32[]{:S(2)}) collective-permute-start(bf16[1152,128]{1,0:T(8,128)(2,1)S(1)} %get-tuple-element.31), channel_id=1, source_target_pairs={{1,2},{3,4},{5,6},{7,8},{9,10},{11,12},{13,14},{2,1},{4,3},{6,5},{... | collective-permute-start | bytes 884744 | tf_op jit(solution)/shard_map/ppermute | solution.py:708
  23.7 29.4 %all-to-all-start.1 = ((bf16[16,64,128]{2,1,0:T(8,128)(2,1)}), bf16[16,64,128]{2,1,0:T(8,128)(2,1)S(1)}, u32[]{:S(2)}, u32[]{:S(2)}) async-start(bf16[16,64,128]{2,1,0:T(8,128)(2,1)} %get-tuple-element.35), calls=%async_computation.1 | async-start | bytes 524288 | tf_op jit(solution)/shard_map/all_to_all | solution.py:704
  40.0 0.7 %copy-start.2 = (bf16[1152,128]{1,0:T(8,128)(2,1)}, bf16[1152,128]{1,0:T(8,128)(2,1)S(1)}, u32[]{:S(2)}) copy-start(bf16[1152,128]{1,0:T(8,128)(2,1)S(1)} %collective-permute-done.a_ref) | copy-start | bytes 884740
  40.0 0.8 %copy-start.3 = (bf16[1152,128]{1,0:T(8,128)(2,1)}, bf16[1152,128]{1,0:T(8,128)(2,1)S(1)}, u32[]{:S(2)}) copy-start(bf16[1152,128]{1,0:T(8,128)(2,1)S(1)} %collective-permute-done.1.b_ref) | copy-start | bytes 884740

commit v2 on v1

--- a/solution.py
+++ b/solution.py
@@ -13,8 +13,8 @@
 smoothing = 0.1
 inv_four_pi = 0.25 / math.pi
 grid_step = 16.0
-UNROLL = 8
-LEAD = UNROLL
+UNROLL = 12
+FAR_UNROLL = 8
 bf16 = jnp.bfloat16
 f32 = jnp.float32
 
@@ -187,7 +187,7 @@
     lane = iota((rows, 128), 1)
     out = jnp.zeros((rows, 128), f32)
     for u in range(UNROLL):
-        place = (iota((rows, 1), 0) * UNROLL + (u - LEAD)).astype(f32)
+        place = (iota((rows, 1), 0) * UNROLL + u).astype(f32)
         begun = start <= place
         target = jnp.sum(jnp.where(begun, 1.0, 0.0), axis=1, keepdims=True) - 1.0
         base = jnp.max(jnp.where(begun, start, 0.0), axis=1, keepdims=True)
@@ -205,7 +205,7 @@
 
 
 def list_rows(slots, leaves):
-    return -(-(leaves * (slots // 2) // UNROLL + 3) // 8) * 8 + 1
+    return -(-(leaves * (slots // 2) // UNROLL + 1) // 8) * 8 + 1
 
 
 def pack_kernel(target_ref, density_ref, out_ref, count_ref, slot_ref, *, peers, per):
@@ -371,26 +371,37 @@
     def item(i, u, part):
         return list_ref[i, part * UNROLL + u]
 
-    def step(i, _):
+    def matrices(i):
+        for u in range(UNROLL):
+            x = jnp.concatenate([fs_ref[item(i, u, 1)], fs_ref[item(i, u, 2)]], axis=0)
+            out = dot(x, ft_ref[item(i, u, 0)])
+            r = lax.rsqrt(out[:, :128])
+            k_ref[u] = ((out[:, 128:] * r) * (r * r)).astype(bf16)
+
+    def apply(i):
         for u in range(UNROLL):
             lhs = jnp.concatenate([dens_ref[item(i, u, 1)], dens_ref[item(i, u, 2)]], axis=1)
             near_ref[item(i, u, 0)] += dot(lhs, k_ref[u])
-        for u in range(UNROLL):
-            x = jnp.concatenate([fs_ref[item(i + 1, u, 1)], fs_ref[item(i + 1, u, 2)]], axis=0)
-            out = dot(x, ft_ref[item(i + 1, u, 0)])
-            r = lax.rsqrt(out[:, :128])
-            k_ref[u] = ((out[:, 128:] * r) * (r * r)).astype(bf16)
+
+    def step(i, _):
+        apply(i - 1)
+        matrices(i)
         return 0
 
-    n = list_ref[list_ref.shape[0] - 1, 0]
-    lax.fori_loop(0, (n + UNROLL - 1) // UNROLL + 1, step, 0)
-
-
-def own_kernel(list_ref, fs_hbm, ft_hbm, own_ref, near_ref, fs_ref, ft_ref, dens_ref, k_ref, sem):
+    steps = jnp.maximum((list_ref[list_ref.shape[0] - 1, 0] + UNROLL - 1) // UNROLL, 1)
+    matrices(0)
+    lax.fori_loop(1, steps, step, 0)
+    apply(steps - 1)
+
+
+def own_kernel(
+    list_hbm, fs_hbm, ft_hbm, own_ref, near_ref, fs_ref, ft_ref, dens_ref, k_ref, list_ref, sem
+):
     leaves = fs_hbm.shape[0]
     half = leaves // 2
     nrhs = 32
     copies = [
+        pltpu.make_async_copy(list_hbm, list_ref, sem.at[3]),
         pltpu.make_async_copy(fs_hbm, fs_ref.at[pl.ds(0, leaves)], sem.at[0]),
         pltpu.make_async_copy(ft_hbm, ft_ref.at[pl.ds(0, leaves)], sem.at[1]),
         pltpu.make_async_copy(fs_hbm.at[0], fs_ref.at[leaves], sem.at[2]),
@@ -407,10 +418,10 @@
 
 
 def leaf_kernel(
-    list_ref, far_list_ref, fs_own_ref, fd_own_ref, ft_hbm, wf_hbm, own_ref, a_ref, b_ref, first_ref,
+    list_hbm, far_list_hbm, fs_own_ref, fd_own_ref, ft_hbm, wf_hbm, own_ref, a_ref, b_ref, first_ref,
     basis_hbm, transfer_hbm,
     near_out, far_out, basis_out_ref, transfer_out_ref,
-    fs_ref, fd_ref, ft_ref, wf_ref, dens_ref, skel_ref, k_ref, g_ref, sem,
+    fs_ref, fd_ref, ft_ref, wf_ref, dens_ref, skel_ref, k_ref, g_ref, list_ref, far_list_ref, sem,
 ):
     leaves = wf_ref.shape[0]
     nrhs = 32
@@ -430,6 +441,10 @@
         pltpu.make_async_copy(basis_hbm, basis_out_ref, sem.at[5]),
         pltpu.make_async_copy(transfer_hbm, transfer_out_ref, sem.at[6]),
     ]
+    copies += [
+        pltpu.make_async_copy(list_hbm, list_ref, sem.at[7]),
+        pltpu.make_async_copy(far_list_hbm, far_list_ref, sem.at[8]),
+    ]
     for c in copies + ahead:
         c.start()
 
@@ -470,42 +485,54 @@
     def far_ids(t):
         return [far_list_ref[t, u] for u in range(slots)]
 
-    def far_step(p, _):
-        done = jnp.maximum(p - 1, 0)
-        e, o = (dot(far_left(far_ids(2 * done + h), skel_ref), g_ref[h]) for h in range(2))
-        even = e[:nrhs] + pltpu.roll(e[nrhs:], 64, 1)
-        odd_ = pltpu.roll(o[:nrhs], 64, 1) + o[nrhs:]
-        far_out[done] = jnp.where(left, even, odd_)
-        for h in range(2):
-            t = 2 * jnp.minimum(p, half - 1) + h
-            ids = far_ids(t)
+    def far_matrices(p):
+        for h in range(FAR_UNROLL):
+            ids = far_ids(FAR_UNROLL * p + h)
             x = [
                 jnp.where(left64, fd_ref[ids[j]], fd_ref[ids[j + 1]]) for j in range(0, slots, 2)
             ]
-            out = dot(jnp.concatenate(x, axis=0), wf_ref[t])
+            out = dot(jnp.concatenate(x, axis=0), wf_ref[FAR_UNROLL * p + h])
             g_ref[h] = (lax.rsqrt(out) * inv_four_pi).astype(bf16)
+
+    def far_apply(p):
+        for h in range(0, FAR_UNROLL, 2):
+            t = FAR_UNROLL * p + h
+            e, o = (dot(far_left(far_ids(t + k), skel_ref), g_ref[h + k]) for k in range(2))
+            even = e[:nrhs] + pltpu.roll(e[nrhs:], 64, 1)
+            odd_ = pltpu.roll(o[:nrhs], 64, 1) + o[nrhs:]
+            far_out[(FAR_UNROLL // 2) * p + h // 2] = jnp.where(left, even, odd_)
+
+    def far_step(p, _):
+        far_apply(p - 1)
+        far_matrices(p)
         return 0
 
-    lax.fori_loop(0, half + 1, far_step, 0)
+    far_steps = leaves // FAR_UNROLL
+    far_matrices(0)
+    lax.fori_loop(1, far_steps, far_step, 0)
+    far_apply(far_steps - 1)
     for c in ahead:
         c.wait()
 
 
 def node_kernel(
-    list_ref, near_ref, far_ref, skel_ref, gn_ref, transfer_ref, basis_ref,
-    out_ref,
-    all_ref,
+    list_hbm, near_ref, far_ref, skel_ref, gn_ref, transfer_ref, basis_ref,
+    out_hbm,
+    all_ref, out_ref, list_ref, sem,
 ):
     nrhs = 32
     nodes_here = gn_ref.shape[0]
     pairs = skel_ref.shape[0] // nrhs
+    listed = pltpu.make_async_copy(list_hbm, list_ref, sem.at[nodes_here])
+    listed.start()
     doubled(skel_ref[...], all_ref, 0)
     all_ref[2 * pairs] = jnp.zeros((nrhs, 128), bf16)
     slots = list_ref.shape[1]
     left = iota((nrhs, 128), 1) < 64
     kids = transfer_ref.shape[2] // 128
-
-    def node(p, _):
+    listed.wait()
+    sent = []
+    for p in range(nodes_here):
         ids = []
         for j in range(slots):
             e = list_ref[p, j]
@@ -522,9 +549,11 @@
             y = dot(both, basis_ref[q])
             out_ref[2 * q] = (near_ref[2 * q] + y[:nrhs]).astype(bf16)
             out_ref[2 * q + 1] = (near_ref[2 * q + 1] + y[nrhs:]).astype(bf16)
-        return 0
-
-    lax.fori_loop(0, nodes_here, node, 0)
+        here = pl.ds(p * 2 * kids, 2 * kids)
+        sent.append(pltpu.make_async_copy(out_ref.at[here], out_hbm.at[here], sem.at[p]))
+        sent[-1].start()
+    for c in sent:
+        c.wait()
 
 
 def vmem():
@@ -535,13 +564,15 @@
     return pl.BlockSpec(memory_space=pltpu.SMEM)
 
 
-def call(kernel, out, in_specs, scratch, name, flops, vmem_mib):
+def call(kernel, out, in_specs, scratch, name, flops, vmem_mib, out_specs=None):
     many = isinstance(out, tuple)
+    if out_specs is None:
+        out_specs = tuple(vmem() for _ in out) if many else vmem()
     return pl.pallas_call(
         kernel,
         out_shape=out,
         in_specs=in_specs,
-        out_specs=tuple(vmem() for _ in out) if many else vmem(),
+        out_specs=out_specs,
         scratch_shapes=scratch,
         name=name,
         cost_estimate=pl.CostEstimate(flops=flops, bytes_accessed=1 << 20, transcendentals=0),
@@ -626,13 +657,14 @@
     return call(
         own_kernel,
         pltpu.VMEM((leaves + 1, 32, 128), f32),
-        [smem(), anywhere, anywhere, vmem()],
+        [anywhere] * 3 + [vmem()],
         [
             pltpu.VMEM((leaves + 1, 128, 128), bf16),
             pltpu.VMEM((leaves + 1, 128, 256), bf16),
             pltpu.VMEM((leaves + 1, 32, 128), bf16),
             pltpu.VMEM((UNROLL, 256, 128), bf16),
-            pltpu.SemaphoreType.DMA((3,)),
+            pltpu.SMEM(own_list.shape, jnp.int32),
+            pltpu.SemaphoreType.DMA((4,)),
         ],
         "own",
         1 << 31,
@@ -652,7 +684,7 @@
             pltpu.VMEM(basis_out.shape, bf16),
             pltpu.VMEM(transfer.shape, bf16),
         ),
-        [smem()] * 2 + [anywhere] * 4 + [vmem()] * 4 + [anywhere] * 2,
+        [anywhere] * 6 + [vmem()] * 4 + [anywhere] * 2,
         [
             pltpu.VMEM((wide + 1, 128, 128), bf16),
             pltpu.VMEM((wide + 1, 64, 128), bf16),
@@ -661,8 +693,10 @@
             pltpu.VMEM((wide + 1, 32, 128), bf16),
             pltpu.VMEM((wide + 1, 32, 128), bf16),
             pltpu.VMEM((UNROLL, 256, 128), bf16),
-            pltpu.VMEM((2, slots * 32, 128), bf16),
-            pltpu.SemaphoreType.DMA((7,)),
+            pltpu.VMEM((FAR_UNROLL, slots * 32, 128), bf16),
+            pltpu.SMEM(halo_list.shape, jnp.int32),
+            pltpu.SMEM(far_list.shape, jnp.int32),
+            pltpu.SemaphoreType.DMA((9,)),
         ],
         "leaves",
         1 << 31,
@@ -677,14 +711,21 @@
     leaves, leaf = 2 * basis_out.shape[0], basis_out.shape[2]
     nrhs = near.shape[1]
     nodes = all_skel.shape[0] // 16
+    anywhere = pl.BlockSpec(memory_space=pl.ANY)
     return call(
         node_kernel,
         jax.ShapeDtypeStruct((leaves, nrhs, leaf), bf16),
-        [smem()] + [vmem()] * 6,
-        [pltpu.VMEM((nodes + 1, nrhs, 128), bf16)],
+        [anywhere] + [vmem()] * 6,
+        [
+            pltpu.VMEM((nodes + 1, nrhs, 128), bf16),
+            pltpu.VMEM((leaves, nrhs, leaf), bf16),
+            pltpu.SMEM(node_list.shape, jnp.int32),
+            pltpu.SemaphoreType.DMA((node_list.shape[0] + 1,)),
+        ],
         "nodes",
         1 << 28,
         8,
+        anywhere,
     )(hbm(node_list), near, far, all_skel, gn, transfer, basis_out)
 
 

time: 57.5 us -> 52.2 us (0.908)
  Pallas kernels: 40.1 us -> 35 us
    pallas_call x1, Pallas kernels: 12.3 us -> 9.56 us  [leaf_fields(): call(leaf_kernel, (pltpu.VMEM((leaves + 1, 32, 128), f32), pltpu.VMEM((le...]
    pallas_call x2, Pallas kernels: 16 us -> 13.7 us  [the longest x1 10.3 us: own_fields(): call(own_kernel, pltpu.VMEM((leaves + 1, 32, 128), f32), [anywhere] * 3 +...]
  transfers between devices with their start and end apart: 4 -> 4, of which waited for: 1 -> 1; matrix products, arithmetic and copies ran while one was open for 0% -> 0% of each run, Pallas kernels for 57% -> 54%
where the time goes in v2:
time: 52.2 us; the launch traced here: 51.9 us
  Pallas kernels  35 us (67%)
  starting transfers between devices  14 us (27%)
  waiting for transfers between devices  1.98 us (4%)
  local copies, waits for them, and re-layouts  0.8 us (2%)
    pallas_call x1, Pallas kernels, own_fields(): call(own_kernel, pltpu.VMEM((leaves + 1, 32, 128), f32), [anywhere] * 3 +...  10.3 us
    pallas_call x1, Pallas kernels, leaf_fields(): call(leaf_kernel, (pltpu.VMEM((leaves + 1, 32, 128), f32), pltpu.VMEM((le...  9.56 us
    pallas_call x1, Pallas kernels, features(): call(feature_kernel, (pltpu.HBM((leaves, 128, 128), bf16), pltpu.HBM((lea...  8.25 us
    all_to_all x1, starting transfers between devices, on_device(): lax.all_to_all(outgoing, AXES, split_axis=0, concat_axis=0, tiled=True)  7.34 us
    all_to_all x1, starting transfers between devices, on_device(): lax.all_to_all(node_out, AXES, split_axis=0, concat_axis=0, tiled=True)  4.1 us
    pallas_call x1, Pallas kernels, finish(): call(node_kernel, jax.ShapeDtypeStruct((leaves, nrhs, leaf), bf16), [anyw...  3.39 us
    ppermute x1, starting transfers between devices, on_device(): got_b = lax.ppermute(to_b, AXES, swap_b)  2.16 us
    pallas_call x1, Pallas kernels, pack(): call(lambda *r: pack_kernel(*r, peers=peers, per=per), jax.ShapeDtypeStru...  2.02 us
  transfers between devices with their start and end apart: 4, of which 1 were waited for; matrix products, arithmetic and copies ran while one was open for 0% of the time, Pallas kernels for 54%

profile of v2, /device:TPU:1, one launch (start us, length us, event | category | flops | bytes accessed | tf_op | source)
XLA Modules:
  0.0 51.9 jit_solution(5768589698550162744)
XLA Ops:
  0.0 2.0 %pack.1 = bf16[16,72,128]{2,1,0:T(8,128)(2,1)} custom-call(s32[32]{0:T(128)} %r_0_.1, bf16[32,32,128]{2,1,0:T(8,128)(2,1)} %r_1_.1), custom_call_target="tpu_custom_call" | custom-call | flops 1048576 | bytes 1048576 | tf_op jit(solution)/shard_map/pack/pallas_call | solution.py:585
  2.0 7.3 %all-to-all-start = ((bf16[16,72,128]{2,1,0:T(8,128)(2,1)}), bf16[16,72,128]{2,1,0:T(8,128)(2,1)S(1)}, u32[]{:S(2)}, u32[]{:S(2)}) async-start(bf16[16,72,128]{2,1,0:T(8,128)(2,1)} %pack.1), calls=%async_computation | async-start | bytes 589824 | tf_op jit(solution)/shard_map/all_to_all | solution.py:742
  9.4 0.0 copy-start
  9.4 0.0 copy-start.1
  9.4 8.3 %features.1 = (bf16[32,128,128]{2,1,0:T(8,128)(2,1)}, bf16[32,64,128]{2,1,0:T(8,128)(2,1)}, bf16[32,128,256]{2,1,0:T(8,128)(2,1)}, bf16[32,128,128]{2,1,0:T(8,12...) custom-call(s32[4,32]{1,0:T(4,128)} %list_hbm.1, ...), custom_call_target="tpu_custom_call" | custom-call | flops 1073741824 | bytes 1048576 | tf_op jit(solution)/shard_map/features/pallas_call | solution.py:601
  17.6 2.0 %all-to-all-done.r_0_ = bf16[16,72,128]{2,1,0:T(8,128)(2,1)S(1)} async-done(((bf16[16,72,128]{2,1,0:T(8,128)(2,1)}), bf16[16,72,128]{2,1,0:T(8,128)(2,1)S(1)}, u32[]{:S(2)}, u32[]{:S(2)}) %all-to-all-start) | async-done | bytes 294944 | tf_op jit(solution)/shard_map/all_to_all | solution.py:742
  19.6 0.0 copy-done
  19.6 0.0 copy-done.1
  19.6 1.5 %skeleton.1 = (bf16[2,1152,128]{2,1,0:T(8,128)(2,1)S(1)}, bf16[1152,128]{1,0:T(8,128)(2,1)}, bf16[1152,128]{1,0:T(8,128)(2,1)S(1)}, bf16[16,64,128]{2,1,0:T(8,128)(2,1)}) custom-call(bf16[16,72,128]{2,1,0:T(8,128)(2,1)S(1)} %all-to-all-done.r_0_, bf16[16,128,128]{2,1,0:T(8,128)(2,1)S(1)} %bitcast.7, bf16[2,128,512]{2,1,0:T(8,128)(2,1)S(1)} %bitcast.8, ...), custom_call_target="tpu_custom_call" | custom-call | flops 67108864 | bytes 1048576 | tf_op jit(solution)/shard_map/skeleton/pallas_call | solution.py:633
  21.1 0.4 collective-permute-start
  21.5 2.2 %collective-permute-start.1 = (bf16[1152,128]{1,0:T(8,128)(2,1)S(1)}, bf16[1152,128]{1,0:T(8,128)(2,1)S(1)}, u32[]{:S(2)}, u32[]{:S(2)}) collective-permute-start(bf16[1152,128]{1,0:T(8,128)(2,1)S(1)} %get-tuple-element.31), channel_id=1, source_target_pairs={{1,2},{3,4},{5,6},{7,8},{9,10},{11,12},{13,14},{2,1},{4,3},{6,5},{... | collective-permute-start | bytes 884744 | tf_op jit(solution)/shard_map/ppermute | solution.py:749
  23.7 4.1 %all-to-all-start.1 = ((bf16[16,64,128]{2,1,0:T(8,128)(2,1)}), bf16[16,64,128]{2,1,0:T(8,128)(2,1)S(1)}, u32[]{:S(2)}, u32[]{:S(2)}) async-start(bf16[16,64,128]{2,1,0:T(8,128)(2,1)} %get-tuple-element.35), calls=%async_computation.1 | async-start | bytes 524288 | tf_op jit(solution)/shard_map/all_to_all | solution.py:745
  27.8 10.3 %own.1.first_ref = f32[33,32,128]{2,1,0:T(8,128)S(1)} custom-call(s32[25,128]{1,0:T(8,128)} %get-tuple-element.32.list_hbm, bf16[32,128,128]{2,1,0:T(8,128)(2,1)} %get-tuple-element.24.fs_hbm.fs_own_ref, bf16[32,128,256]{2,1,0:T(8,128)(2,1)} %get-tuple-element.26.ft_hbm, bf16[2,1152,128]{2,1,0:T(8,128)(2,1)S(1)} %get-tuple-element.29.own_ref), custom_call_target="tpu_custom_call" | custom-call | flops 2147483648 | bytes 1048576 | tf_op jit(solution)/shard_map/own/pallas_call | solution.py:657
  38.1 0.0 collective-permute-done.a_ref
  38.1 0.0 copy-start.2
  38.1 0.0 collective-permute-done.1.b_ref
  38.1 0.0 copy-start.3
  38.1 0.7 %copy-done.2 = bf16[1152,128]{1,0:T(8,128)(2,1)} copy-done((bf16[1152,128]{1,0:T(8,128)(2,1)}, bf16[1152,128]{1,0:T(8,128)(2,1)S(1)}, u32[]{:S(2)}) %copy-start.2) | copy-done | bytes 294936
  38.9 0.1 copy-done.3
  38.9 9.6 %leaves.1 = (f32[33,32,128]{2,1,0:T(8,128)S(1)}, f32[16,32,128]{2,1,0:T(8,128)S(1)}, bf16[16,128,128]{2,1,0:T(8,128)(2,1)S(1)}, bf16[4,64,512]{2,1,0:T(8,128)(2,1)S(1)}) custom-call(s32[25,128]{1,0:T(8,128)} %get-tuple-element.22.list_hbm, s32[32,128]{1,0:T(8,128)} %get-tuple-element.23.far_list_hbm, ...), custom_call_target="tpu_custom_call" | custom-call | flops 2147483648 | bytes 1048576 | tf_op jit(solution)/shard_map/leaves/pallas_call | solution.py:679
  48.5 0.0 all-to-all-done.1
  48.5 3.4 %nodes.1 = bf16[32,32,128]{2,1,0:T(8,128)(2,1)} custom-call(s32[4,32]{1,0:T(4,128)} %list_hbm.1, f32[33,32,128]{2,1,0:T(8,128)S(1)} %get-tuple-element.33.near_ref, f32[16,32,128]{2,1,0:T(8,128)S(1)} %get-tuple-element.34.far_ref, bf16[1024,128]{1,0:T(8,128)(2,1)S(1)} %bitcast.6, bf16[4,1024,128]{2,1,0:T(8,128)(2,1)S(1)} %get-tuple-element.36.gn_ref, ...), custom_call_target="tpu_custom_call" | custom-call | flops 268435456 | bytes 1048576 | tf_op jit(solution)/shard_map/nodes/pallas_call | solution.py:715
Async XLA Ops:
  2.0 17.6 %all-to-all-start = ((bf16[16,72,128]{2,1,0:T(8,128)(2,1)}), bf16[16,72,128]{2,1,0:T(8,128)(2,1)S(1)}, u32[]{:S(2)}, u32[]{:S(2)}) async-start(bf16[16,72,128]{2,1,0:T(8,128)(2,1)} %pack.1), calls=%async_computation | async-start | bytes 589824 | tf_op jit(solution)/shard_map/all_to_all | solution.py:742
  9.4 10.2 %copy-start = (bf16[32,64,128]{2,1,0:T(8,128)(2,1)S(1)}, bf16[32,64,128]{2,1,0:T(8,128)(2,1)}, u32[]{:S(2)}) copy-start(bf16[32,64,128]{2,1,0:T(8,128)(2,1)} %param.16) | copy-start | bytes 1572868
  9.4 10.2 %copy-start.1 = (bf16[4,64,512]{2,1,0:T(8,128)(2,1)S(1)}, bf16[4,64,512]{2,1,0:T(8,128)(2,1)}, u32[]{:S(2)}) copy-start(bf16[4,64,512]{2,1,0:T(8,128)(2,1)} %transfer_hbm.1) | copy-start | bytes 786436
  21.1 17.0 %collective-permute-start = (bf16[1152,128]{1,0:T(8,128)(2,1)}, bf16[1152,128]{1,0:T(8,128)(2,1)S(1)}, u32[]{:S(2)}, u32[]{:S(2)}) collective-permute-start(bf16[1152,128]{1,0:T(8,128)(2,1)} %get-tuple-element.30), channel_id=1, source_target_pairs={{0,1},{1,0},{2,3},{3,2},{4,5},{5,4},{6,7},{7,6},{8,9},{9,8},{10,11... | collective-permute-start | bytes 884744 | tf_op jit(solution)/shard_map/ppermute | solution.py:748
  21.5 16.6 %collective-permute-start.1 = (bf16[1152,128]{1,0:T(8,128)(2,1)S(1)}, bf16[1152,128]{1,0:T(8,128)(2,1)S(1)}, u32[]{:S(2)}, u32[]{:S(2)}) collective-permute-start(bf16[1152,128]{1,0:T(8,128)(2,1)S(1)} %get-tuple-element.31), channel_id=1, source_target_pairs={{1,2},{3,4},{5,6},{7,8},{9,10},{11,12},{13,14},{2,1},{4,3},{6,5},{... | collective-permute-start | bytes 884744 | tf_op jit(solution)/shard_map/ppermute | solution.py:749
  23.7 24.8 %all-to-all-start.1 = ((bf16[16,64,128]{2,1,0:T(8,128)(2,1)}), bf16[16,64,128]{2,1,0:T(8,128)(2,1)S(1)}, u32[]{:S(2)}, u32[]{:S(2)}) async-start(bf16[16,64,128]{2,1,0:T(8,128)(2,1)} %get-tuple-element.35), calls=%async_computation.1 | async-start | bytes 524288 | tf_op jit(solution)/shard_map/all_to_all | solution.py:745
  38.1 0.7 %copy-start.2 = (bf16[1152,128]{1,0:T(8,128)(2,1)}, bf16[1152,128]{1,0:T(8,128)(2,1)S(1)}, u32[]{:S(2)}) copy-start(bf16[1152,128]{1,0:T(8,128)(2,1)S(1)} %collective-permute-done.a_ref) | copy-start | bytes 884740
  38.1 0.8 %copy-start.3 = (bf16[1152,128]{1,0:T(8,128)(2,1)}, bf16[1152,128]{1,0:T(8,128)(2,1)S(1)}, u32[]{:S(2)}) copy-start(bf16[1152,128]{1,0:T(8,128)(2,1)S(1)} %collective-permute-done.1.b_ref) | copy-start | bytes 884740

commit v3 on v2

--- a/solution.py
+++ b/solution.py
@@ -418,10 +418,13 @@
 
 
 def leaf_kernel(
-    list_hbm, far_list_hbm, fs_own_ref, fd_own_ref, ft_hbm, wf_hbm, own_ref, a_ref, b_ref, first_ref,
-    basis_hbm, transfer_hbm,
-    near_out, far_out, basis_out_ref, transfer_out_ref,
-    fs_ref, fd_ref, ft_ref, wf_ref, dens_ref, skel_ref, k_ref, g_ref, list_ref, far_list_ref, sem,
+    list_hbm, far_list_hbm, node_list_hbm, fs_own_ref, fd_own_ref, ft_hbm, wf_hbm, basis_hbm, transfer_hbm,
+    own_ref, a_any, b_any, first_ref, all_skel_ref, gn_ref,
+    out_hbm,
+    a_ref, b_ref,
+    fs_ref, fd_ref, ft_ref, wf_ref, basis_ref, transfer_ref,
+    dens_ref, skel_ref, all_ref, near_ref, down_ref, far_ref, out_ref, k_ref, g_ref,
+    list_ref, far_list_ref, node_list_ref, sem, out_sem,
 ):
     leaves = wf_ref.shape[0]
     nrhs = 32
@@ -437,16 +440,25 @@
         pltpu.make_async_copy(fs_own_ref.at[0], fs_ref.at[wide], sem.at[3]),
         pltpu.make_async_copy(fd_own_ref.at[0], fd_ref.at[wide], sem.at[4]),
     ]
-    ahead = [
-        pltpu.make_async_copy(basis_hbm, basis_out_ref, sem.at[5]),
-        pltpu.make_async_copy(transfer_hbm, transfer_out_ref, sem.at[6]),
+    copies += [
+        pltpu.make_async_copy(list_hbm, list_ref, sem.at[5]),
+        pltpu.make_async_copy(far_list_hbm, far_list_ref, sem.at[6]),
+        pltpu.make_async_copy(node_list_hbm, node_list_ref, sem.at[7]),
     ]
-    copies += [
-        pltpu.make_async_copy(list_hbm, list_ref, sem.at[7]),
-        pltpu.make_async_copy(far_list_hbm, far_list_ref, sem.at[8]),
+    later = [
+        copies.pop(2),
+        copies.pop(0),
+        pltpu.make_async_copy(basis_hbm, basis_ref, sem.at[8]),
+        pltpu.make_async_copy(transfer_hbm, transfer_ref, sem.at[9]),
     ]
-    for c in copies + ahead:
+    arrived = [
+        pltpu.make_async_copy(a_any, a_ref, sem.at[10]),
+        pltpu.make_async_copy(b_any, b_ref, sem.at[11]),
+    ]
+    for c in arrived + copies + later:
         c.start()
+    for c in arrived:
+        c.wait()
 
     base = half * nrhs + (half // 2) * nrhs
     for right, k in ((False, 0), (True, REACH + leaves)):
@@ -474,10 +486,27 @@
     fill(lambda at, n: jnp.where(odd, b_ref[at : at + n, :], a_ref[at : at + n, :]), REACH + leaves)
     dens_ref[wide] = jnp.zeros((nrhs, 128), bf16)
     skel_ref[wide] = jnp.zeros((nrhs, 128), bf16)
-    near_out[...] = first_ref[...]
+    near_ref[...] = first_ref[...]
+    pairs = all_skel_ref.shape[0] // nrhs
+    doubled(all_skel_ref[...], all_ref, 0)
+    all_ref[2 * pairs] = jnp.zeros((nrhs, 128), bf16)
     for c in copies:
         c.wait()
-    near_pairs(list_ref, fs_ref, ft_ref, dens_ref, k_ref, near_out)
+    near_pairs(list_ref, fs_ref, ft_ref, dens_ref, k_ref, near_ref)
+    for c in later:
+        c.wait()
+
+    kids = transfer_ref.shape[2] // 128
+    for p in range(gn_ref.shape[0]):
+        ids = []
+        for j in range(node_list_ref.shape[1]):
+            e = node_list_ref[p, j]
+            ids.append(jnp.where(e < 0, 2 * pairs, e))
+        acc = dot(far_left(ids, all_ref), gn_ref[p])
+        x = acc[:nrhs] + pltpu.roll(acc[nrhs:], 64, 1)
+        down = dot(x[:, :64].astype(bf16), transfer_ref[p])
+        for c in range(kids):
+            down_ref[p * kids + c] = down[:, c * 128 : (c + 1) * 128]
 
     left = iota((nrhs, 128), 1) < 64
     left64 = iota((64, 128), 1) < 64
@@ -500,59 +529,32 @@
             e, o = (dot(far_left(far_ids(t + k), skel_ref), g_ref[h + k]) for k in range(2))
             even = e[:nrhs] + pltpu.roll(e[nrhs:], 64, 1)
             odd_ = pltpu.roll(o[:nrhs], 64, 1) + o[nrhs:]
-            far_out[(FAR_UNROLL // 2) * p + h // 2] = jnp.where(left, even, odd_)
-
-    def far_step(p, _):
-        far_apply(p - 1)
-        far_matrices(p)
-        return 0
-
-    far_steps = leaves // FAR_UNROLL
-    far_matrices(0)
-    lax.fori_loop(1, far_steps, far_step, 0)
-    far_apply(far_steps - 1)
-    for c in ahead:
-        c.wait()
-
-
-def node_kernel(
-    list_hbm, near_ref, far_ref, skel_ref, gn_ref, transfer_ref, basis_ref,
-    out_hbm,
-    all_ref, out_ref, list_ref, sem,
-):
-    nrhs = 32
-    nodes_here = gn_ref.shape[0]
-    pairs = skel_ref.shape[0] // nrhs
-    listed = pltpu.make_async_copy(list_hbm, list_ref, sem.at[nodes_here])
-    listed.start()
-    doubled(skel_ref[...], all_ref, 0)
-    all_ref[2 * pairs] = jnp.zeros((nrhs, 128), bf16)
-    slots = list_ref.shape[1]
-    left = iota((nrhs, 128), 1) < 64
-    kids = transfer_ref.shape[2] // 128
-    listed.wait()
-    sent = []
-    for p in range(nodes_here):
-        ids = []
-        for j in range(slots):
-            e = list_ref[p, j]
-            ids.append(jnp.where(e < 0, 2 * pairs, e))
-        acc = dot(far_left(ids, all_ref), gn_ref[p])
-        x = acc[:nrhs] + pltpu.roll(acc[nrhs:], 64, 1)
-        down = dot(x[:, :64].astype(bf16), transfer_ref[p])
-        for c in range(kids):
-            q = p * kids + c
-            local = (far_ref[q] + down[:, c * 128 : (c + 1) * 128]).astype(bf16).astype(f32)
+            far_ref[(FAR_UNROLL // 2) * p + h // 2] = jnp.where(left, even, odd_)
+
+    def finish(p):
+        for q in range(FAR_UNROLL // 2 * p, FAR_UNROLL // 2 * (p + 1)):
+            local = (far_ref[q] + down_ref[q]).astype(bf16).astype(f32)
             both = jnp.concatenate(
                 [jnp.where(left, local, 0.0), jnp.where(left, 0.0, local)], axis=0
             ).astype(bf16)
             y = dot(both, basis_ref[q])
             out_ref[2 * q] = (near_ref[2 * q] + y[:nrhs]).astype(bf16)
             out_ref[2 * q + 1] = (near_ref[2 * q + 1] + y[nrhs:]).astype(bf16)
-        here = pl.ds(p * 2 * kids, 2 * kids)
-        sent.append(pltpu.make_async_copy(out_ref.at[here], out_hbm.at[here], sem.at[p]))
-        sent[-1].start()
-    for c in sent:
+        here = pl.ds(p * FAR_UNROLL, FAR_UNROLL)
+        written = pltpu.make_async_copy(out_ref.at[here], out_hbm.at[here], out_sem.at[p])
+        written.start()
+        return written
+
+    far_steps = leaves // FAR_UNROLL
+    written = []
+    for p in range(far_steps + 2):
+        if p >= 2:
+            written.append(finish(p - 2))
+        if 1 <= p <= far_steps:
+            far_apply(p - 1)
+        if p < far_steps:
+            far_matrices(p)
+    for c in written:
         c.wait()
 
 
@@ -634,8 +636,8 @@
         lambda *r: skeleton_kernel(*r, per=per),
         (
             pltpu.VMEM((2, rows, 128), bf16),
-            shape((rows, 128), bf16),
-            shape((rows, 128), bf16),
+            pltpu.HBM((rows, 128), bf16),
+            pltpu.HBM((rows, 128), bf16),
             shape((peers, nodes_here // 2 * 32, 128), bf16),
         ),
         [vmem()] * 4,
@@ -672,61 +674,50 @@
     )(hbm(own_list), hbm(fs), hbm(ft), own)
 
 
-def leaf_fields(slots, halo_list, far_list, fs, fd, ft, wf, own, got_a, got_b, first, basis_out, transfer):
+def leaf_fields(
+    far_slots, halo_list, far_list, node_list, fs, fd, ft, wf, basis_out, transfer, own, got_a, got_b, first, all_skel, gn
+):
     leaves = ft.shape[0]
     wide = leaves + 2 * REACH
+    nodes = all_skel.shape[0] // 16
     anywhere = pl.BlockSpec(memory_space=pl.ANY)
+    basis_out = basis_out.reshape(leaves // 2, 128, -1)
     return call(
         leaf_kernel,
-        (
-            pltpu.VMEM((leaves + 1, 32, 128), f32),
-            pltpu.VMEM((leaves // 2, 32, 128), f32),
-            pltpu.VMEM(basis_out.shape, bf16),
-            pltpu.VMEM(transfer.shape, bf16),
-        ),
-        [anywhere] * 6 + [vmem()] * 4 + [anywhere] * 2,
+        jax.ShapeDtypeStruct((leaves, 32, 128), bf16),
+        [anywhere] * 9 + [vmem()] + [anywhere] * 2 + [vmem()] * 3,
         [
+            pltpu.VMEM(got_a.shape, bf16),
+            pltpu.VMEM(got_a.shape, bf16),
             pltpu.VMEM((wide + 1, 128, 128), bf16),
             pltpu.VMEM((wide + 1, 64, 128), bf16),
             pltpu.VMEM((leaves + 1, 128, 256), bf16),
             pltpu.VMEM((leaves, 128, 128), bf16),
+            pltpu.VMEM(basis_out.shape, bf16),
+            pltpu.VMEM(transfer.shape, bf16),
             pltpu.VMEM((wide + 1, 32, 128), bf16),
             pltpu.VMEM((wide + 1, 32, 128), bf16),
+            pltpu.VMEM((nodes + 1, 32, 128), bf16),
+            pltpu.VMEM((leaves + 1, 32, 128), f32),
+            pltpu.VMEM((leaves // 2, 32, 128), f32),
+            pltpu.VMEM((leaves // 2, 32, 128), f32),
+            pltpu.VMEM((leaves, 32, 128), bf16),
             pltpu.VMEM((UNROLL, 256, 128), bf16),
-            pltpu.VMEM((FAR_UNROLL, slots * 32, 128), bf16),
+            pltpu.VMEM((FAR_UNROLL, gn.shape[1] // node_list.shape[1] * far_slots, 128), bf16),
             pltpu.SMEM(halo_list.shape, jnp.int32),
             pltpu.SMEM(far_list.shape, jnp.int32),
-            pltpu.SemaphoreType.DMA((9,)),
+            pltpu.SMEM(node_list.shape, jnp.int32),
+            pltpu.SemaphoreType.DMA((12,)),
+            pltpu.SemaphoreType.DMA((leaves // FAR_UNROLL,)),
         ],
         "leaves",
         1 << 31,
-        20,
+        24,
+        anywhere,
     )(
-        hbm(halo_list), hbm(far_list), hbm(fs), hbm(fd), hbm(ft), hbm(wf), own, hbm(got_a), hbm(got_b), first,
-        hbm(basis_out), hbm(transfer),
+        *map(hbm, (halo_list, far_list, node_list, fs, fd, ft, wf, basis_out, transfer)),
+        own, got_a, got_b, first, all_skel, gn,
     )
-
-
-def finish(node_list, near, far, all_skel, gn, transfer, basis_out):
-    leaves, leaf = 2 * basis_out.shape[0], basis_out.shape[2]
-    nrhs = near.shape[1]
-    nodes = all_skel.shape[0] // 16
-    anywhere = pl.BlockSpec(memory_space=pl.ANY)
-    return call(
-        node_kernel,
-        jax.ShapeDtypeStruct((leaves, nrhs, leaf), bf16),
-        [anywhere] + [vmem()] * 6,
-        [
-            pltpu.VMEM((nodes + 1, nrhs, 128), bf16),
-            pltpu.VMEM((leaves, nrhs, leaf), bf16),
-            pltpu.SMEM(node_list.shape, jnp.int32),
-            pltpu.SemaphoreType.DMA((node_list.shape[0] + 1,)),
-        ],
-        "nodes",
-        1 << 28,
-        8,
-        anywhere,
-    )(hbm(node_list), near, far, all_skel, gn, transfer, basis_out)
 
 
 def hbm(x):
@@ -748,11 +739,10 @@
     got_a = lax.ppermute(to_a, AXES, swap_a)
     got_b = lax.ppermute(to_b, AXES, swap_b)
     first = own_fields(own_pairs, fs, ft, own)
-    near, far, basis_out, transfer = leaf_fields(
-        near_list.shape[1], halo_pairs, far_rows, fs, fd, ft, wf, own, got_a, got_b, first,
-        basis_out.reshape(basis_out.shape[0] // 2, 128, -1), transfer,
+    return leaf_fields(
+        far_list.shape[1], halo_pairs, far_rows, node_list, fs, fd, ft, wf, basis_out, transfer, own, got_a, got_b,
+        first, all_skel.reshape(-1, 128), gn,
     )
-    return finish(node_list, near, far, all_skel.reshape(-1, 128), gn, transfer, basis_out)
 
 
 def solution(mesh):

time: 52.2 us -> 50.3 us (0.964)
  Pallas kernels: 35 us -> 33.3 us
  starting transfers between devices: 14 us -> 15.1 us
  local copies, waits for them, and re-layouts: 0.8 us -> 0.01 us
    pallas_call x2 -> x1, Pallas kernels: 12.9 us -> 10.4 us  [leaf_fields(): call(leaf_kernel, jax.ShapeDtypeStruct((leaves, 32, 128), bf16), [anywher...]
    ppermute x1, starting transfers between devices: 2.16 us -> 3.48 us  [on_device(): got_b = lax.ppermute(to_b, AXES, swap_b)]
    unnamed x8 -> x4, local copies, waits for them, and re-layouts: 0.8 us -> 0.01 us
    pallas_call x1, Pallas kernels: 10.3 us -> 11 us  [own_fields(): call(own_kernel, pltpu.VMEM((leaves + 1, 32, 128), f32), [anywhere] * 3 +...]
  transfers between devices with their start and end apart: 4 -> 4, of which waited for: 1 -> 1; matrix products, arithmetic and copies ran while one was open for 0% -> 0% of each run, Pallas kernels for 54% -> 38%
where the time goes in v3:
time: 50.3 us; the launch traced here: 50.4 us
  Pallas kernels  33.3 us (66%)
  starting transfers between devices  15.1 us (30%)
  waiting for transfers between devices  1.98 us (4%)
    pallas_call x1, Pallas kernels, own_fields(): call(own_kernel, pltpu.VMEM((leaves + 1, 32, 128), f32), [anywhere] * 3 +...  11 us
    pallas_call x1, Pallas kernels, leaf_fields(): call(leaf_kernel, jax.ShapeDtypeStruct((leaves, 32, 128), bf16), [anywher...  10.4 us
    pallas_call x1, Pallas kernels, features(): call(feature_kernel, (pltpu.HBM((leaves, 128, 128), bf16), pltpu.HBM((lea...  8.25 us
    all_to_all x1, starting transfers between devices, on_device(): lax.all_to_all(outgoing, AXES, split_axis=0, concat_axis=0, tiled=True)  7.34 us
    all_to_all x1, starting transfers between devices, on_device(): lax.all_to_all(node_out, AXES, split_axis=0, concat_axis=0, tiled=True)  4.07 us
    ppermute x1, starting transfers between devices, on_device(): got_b = lax.ppermute(to_b, AXES, swap_b)  3.48 us
    pallas_call x1, Pallas kernels, pack(): call(lambda *r: pack_kernel(*r, peers=peers, per=per), jax.ShapeDtypeStru...  2 us
    all_to_all x1, waiting for transfers between devices, on_device(): lax.all_to_all(outgoing, AXES, split_axis=0, concat_axis=0, tiled=True)  1.97 us
  transfers between devices with their start and end apart: 4, of which 1 were waited for; matrix products, arithmetic and copies ran while one was open for 0% of the time, Pallas kernels for 38%

profile of v3, /device:TPU:1, one launch (start us, length us, event | category | flops | bytes accessed | tf_op | source)
XLA Modules:
  0.0 50.4 jit_solution(15495766442522756568)
XLA Ops:
  0.0 2.0 %pack.1 = bf16[16,72,128]{2,1,0:T(8,128)(2,1)} custom-call(s32[32]{0:T(128)} %r_0_.1, bf16[32,32,128]{2,1,0:T(8,128)(2,1)} %r_1_.1), custom_call_target="tpu_custom_call" | custom-call | flops 1048576 | bytes 1048576 | tf_op jit(solution)/shard_map/pack/pallas_call | solution.py:587
  2.0 7.3 %all-to-all-start = ((bf16[16,72,128]{2,1,0:T(8,128)(2,1)}), bf16[16,72,128]{2,1,0:T(8,128)(2,1)S(1)}, u32[]{:S(2)}, u32[]{:S(2)}) async-start(bf16[16,72,128]{2,1,0:T(8,128)(2,1)} %pack.1), calls=%async_computation | async-start | bytes 589824 | tf_op jit(solution)/shard_map/all_to_all | solution.py:733
  9.3 0.0 copy-start
  9.3 0.0 copy-start.1
  9.4 8.3 %features.1 = (bf16[32,128,128]{2,1,0:T(8,128)(2,1)}, bf16[32,64,128]{2,1,0:T(8,128)(2,1)}, bf16[32,128,256]{2,1,0:T(8,128)(2,1)}, bf16[32,128,128]{2,1,0:T(8,12...) custom-call(s32[4,32]{1,0:T(4,128)} %node_list_hbm.1, ...), custom_call_target="tpu_custom_call" | custom-call | flops 1073741824 | bytes 1048576 | tf_op jit(solution)/shard_map/features/pallas_call | solution.py:603
  17.6 2.0 %all-to-all-done.r_0_ = bf16[16,72,128]{2,1,0:T(8,128)(2,1)S(1)} async-done(((bf16[16,72,128]{2,1,0:T(8,128)(2,1)}), bf16[16,72,128]{2,1,0:T(8,128)(2,1)S(1)}, u32[]{:S(2)}, u32[]{:S(2)}) %all-to-all-start) | async-done | bytes 294944 | tf_op jit(solution)/shard_map/all_to_all | solution.py:733
  19.6 0.0 copy-done
  19.6 0.0 copy-done.1
  19.6 1.6 %skeleton.1 = (bf16[2,1152,128]{2,1,0:T(8,128)(2,1)S(1)}, bf16[1152,128]{1,0:T(8,128)(2,1)}, bf16[1152,128]{1,0:T(8,128)(2,1)}, bf16[16,64,128]{2,1,0:T(8,128)(2,1)}) custom-call(bf16[16,72,128]{2,1,0:T(8,128)(2,1)S(1)} %all-to-all-done.r_0_, bf16[16,128,128]{2,1,0:T(8,128)(2,1)S(1)} %bitcast.8, bf16[2,128,512]{2,1,0:T(8,128)(2,1)S(1)} %bitcast.6, ...), custom_call_target="tpu_custom_call" | custom-call | flops 67108864 | bytes 1048576 | tf_op jit(solution)/shard_map/skeleton/pallas_call | solution.py:635
  21.2 4.1 %all-to-all-start.1 = ((bf16[16,64,128]{2,1,0:T(8,128)(2,1)}), bf16[16,64,128]{2,1,0:T(8,128)(2,1)S(1)}, u32[]{:S(2)}, u32[]{:S(2)}) async-start(bf16[16,64,128]{2,1,0:T(8,128)(2,1)} %get-tuple-element.29), calls=%async_computation.1 | async-start | bytes 524288 | tf_op jit(solution)/shard_map/all_to_all | solution.py:736
  25.3 0.2 collective-permute-start
  25.4 3.5 %collective-permute-start.1 = (bf16[1152,128]{1,0:T(8,128)(2,1)}, bf16[1152,128]{1,0:T(8,128)(2,1)S(1)}, u32[]{:S(2)}, u32[]{:S(2)}) collective-permute-start(bf16[1152,128]{1,0:T(8,128)(2,1)} %get-tuple-element.27), channel_id=1, source_target_pairs={{1,2},{3,4},{5,6},{7,8},{9,10},{11,12},{13,14},{2,1},{4,3},{6,5},{... | collective-permute-start | bytes 884744 | tf_op jit(solution)/shard_map/ppermute | solution.py:740
  28.9 11.0 %own.1.first_ref = f32[33,32,128]{2,1,0:T(8,128)S(1)} custom-call(s32[25,128]{1,0:T(8,128)} %get-tuple-element.28.list_hbm, bf16[32,128,128]{2,1,0:T(8,128)(2,1)} %get-tuple-element.20.fs_hbm.fs_own_ref, bf16[32,128,256]{2,1,0:T(8,128)(2,1)} %get-tuple-element.22.ft_hbm, bf16[2,1152,128]{2,1,0:T(8,128)(2,1)S(1)} %get-tuple-element.25.own_ref), custom_call_target="tpu_custom_call" | custom-call | flops 2147483648 | bytes 1048576 | tf_op jit(solution)/shard_map/own/pallas_call | solution.py:659
  39.9 0.0 collective-permute-done.a_any
  39.9 0.0 collective-permute-done.1.b_any
  39.9 0.0 all-to-all-done.1
  40.0 10.4 %leaves.1 = bf16[32,32,128]{2,1,0:T(8,128)(2,1)} custom-call(s32[25,128]{1,0:T(8,128)} %get-tuple-element.18.list_hbm, s32[32,128]{1,0:T(8,128)} %get-tuple-element.19.far_list_hbm, s32[4,32]{1,0:T(4,128)} %node_list_hbm.1, bf16[32,128,128]{2,1,0:T(8,128)(2,1)} %get-tuple-element.20.fs_hbm.fs_own_ref, bf16[32,64,128]{2,1,0:T(8,128)(2,1)} %get-tuple-element.21.fd_own_ref, ...), custom_call_target="tpu_custom_call" | custom-call | flops 2147483648 | bytes 1048576 | tf_op jit(solution)/shard_map/leaves/pallas_call | solution.py:685
Async XLA Ops:
  2.0 17.6 %all-to-all-start = ((bf16[16,72,128]{2,1,0:T(8,128)(2,1)}), bf16[16,72,128]{2,1,0:T(8,128)(2,1)S(1)}, u32[]{:S(2)}, u32[]{:S(2)}) async-start(bf16[16,72,128]{2,1,0:T(8,128)(2,1)} %pack.1), calls=%async_computation | async-start | bytes 589824 | tf_op jit(solution)/shard_map/all_to_all | solution.py:733
  9.3 10.2 %copy-start = (bf16[4,64,512]{2,1,0:T(8,128)(2,1)S(1)}, bf16[4,64,512]{2,1,0:T(8,128)(2,1)}, u32[]{:S(2)}) copy-start(bf16[4,64,512]{2,1,0:T(8,128)(2,1)} %transfer_hbm.1) | copy-start | bytes 786436
  9.3 10.2 %copy-start.1 = (bf16[32,64,128]{2,1,0:T(8,128)(2,1)S(1)}, bf16[32,64,128]{2,1,0:T(8,128)(2,1)}, u32[]{:S(2)}) copy-start(bf16[32,64,128]{2,1,0:T(8,128)(2,1)} %param.16) | copy-start | bytes 1572868
  21.2 18.7 %all-to-all-start.1 = ((bf16[16,64,128]{2,1,0:T(8,128)(2,1)}), bf16[16,64,128]{2,1,0:T(8,128)(2,1)S(1)}, u32[]{:S(2)}, u32[]{:S(2)}) async-start(bf16[16,64,128]{2,1,0:T(8,128)(2,1)} %get-tuple-element.29), calls=%async_computation.1 | async-start | bytes 524288 | tf_op jit(solution)/shard_map/all_to_all | solution.py:736
  25.3 14.7 %collective-permute-start = (bf16[1152,128]{1,0:T(8,128)(2,1)}, bf16[1152,128]{1,0:T(8,128)(2,1)S(1)}, u32[]{:S(2)}, u32[]{:S(2)}) collective-permute-start(bf16[1152,128]{1,0:T(8,128)(2,1)} %get-tuple-element.26), channel_id=1, source_target_pairs={{0,1},{1,0},{2,3},{3,2},{4,5},{5,4},{6,7},{7,6},{8,9},{9,8},{10,11... | collective-permute-start | bytes 884744 | tf_op jit(solution)/shard_map/ppermute | solution.py:739
  25.4 14.5 %collective-permute-start.1 = (bf16[1152,128]{1,0:T(8,128)(2,1)}, bf16[1152,128]{1,0:T(8,128)(2,1)S(1)}, u32[]{:S(2)}, u32[]{:S(2)}) collective-permute-start(bf16[1152,128]{1,0:T(8,128)(2,1)} %get-tuple-element.27), channel_id=1, source_target_pairs={{1,2},{3,4},{5,6},{7,8},{9,10},{11,12},{13,14},{2,1},{4,3},{6,5},{... | collective-permute-start | bytes 884744 | tf_op jit(solution)/shard_map/ppermute | solution.py:740

commit v4 on v3

--- a/solution.py
+++ b/solution.py
@@ -7,6 +7,7 @@
 from jax.experimental.pallas import tpu as pltpu
 from jax.sharding import PartitionSpec as P
 
+
 REACH = 16
 AXES = ("row", "col")
 
@@ -14,6 +15,7 @@
 inv_four_pi = 0.25 / math.pi
 grid_step = 16.0
 UNROLL = 12
+AHEAD = 2
 FAR_UNROLL = 8
 bf16 = jnp.bfloat16
 f32 = jnp.float32
@@ -97,7 +99,7 @@
         ]
 
     def source_normal(self):
-        m0, m1, m2 = self.m
+        m0, m1, _ = self.m
         u0, u1, u2 = (pltpu.roll(x, 5, 0) for x in self.m)
         q0, q1, q2 = self.q
         return [
@@ -214,7 +216,7 @@
         count_ref[d] = 0
     for k in range(leaves):
         t = target_ref[k]
-        d = t // leaves
+        d = lax.div(t, leaves)
         c = count_ref[d]
         count_ref[d] = c + 1
         slot_ref[d * per + c] = t - d * leaves
@@ -229,10 +231,10 @@
 
 def feature_kernel(
     node_list_ref, geo_ref, node_ref, near_ref, far_ref,
-    fs_ref, fd_ref, ft_ref, wf_ref, split_ref, gn_ref, own_list_ref, halo_list_ref, far_list_ref,
-    pad_ref, npad_ref, fsn_ref, wfn_ref,
+    fs_ref, fd_ref, ft_ref, wf_ref, split_ref, gn_ref, own_list_ref, halo_list_ref, far_list_ref, ready_ref,
+    pad_ref, npad_ref, fsn_ref, wfn_ref, rows_ref, sem,
 ):
-    leaves = fs_ref.shape[0]
+    leaves = fd_ref.shape[0]
     nodes_here = wfn_ref.shape[0]
     slots = near_ref.shape[0]
     index = lax.axis_index(AXES)
@@ -245,6 +247,8 @@
     entries = near_ref[...]
     local = (entries >= index * leaves) & (entries < (index + 1) * leaves)
     items(*compact(jnp.where(local, entries, -1), index * leaves, leaves), leaves, own_list_ref)
+    listed = pltpu.make_async_copy(own_list_ref, rows_ref, sem.at[0])
+    listed.start()
     items(*compact(jnp.where(local, -1, entries), first, wide), wide, halo_list_ref)
     far, _ = compact(far_ref[...], first, wide)
     same = jnp.where(iota((leaves, leaves), 0) == iota((leaves, leaves), 1), 1.0, 0.0).astype(bf16)
@@ -267,6 +271,8 @@
         return 0
 
     lax.fori_loop(0, leaves, leaf_step, 0, unroll=4)
+    fs_ref[leaves] = fs_ref[0]
+    ft_ref[leaves] = ft_ref[0]
 
     def split_step(l, _):
         parts = []
@@ -304,6 +310,9 @@
         return 0
 
     lax.fori_loop(0, nodes_here, node_field, 0)
+    listed.wait()
+    for i in range(AHEAD):
+        pair_matrices(rows_ref, i, fs_ref, ft_ref, ready_ref, i * UNROLL)
 
 
 def skeleton_kernel(
@@ -367,44 +376,46 @@
     return jnp.concatenate(cols, axis=1)
 
 
-def near_pairs(list_ref, fs_ref, ft_ref, dens_ref, k_ref, near_ref):
-    def item(i, u, part):
-        return list_ref[i, part * UNROLL + u]
-
-    def matrices(i):
-        for u in range(UNROLL):
-            x = jnp.concatenate([fs_ref[item(i, u, 1)], fs_ref[item(i, u, 2)]], axis=0)
-            out = dot(x, ft_ref[item(i, u, 0)])
-            r = lax.rsqrt(out[:, :128])
-            k_ref[u] = ((out[:, 128:] * r) * (r * r)).astype(bf16)
-
-    def apply(i):
-        for u in range(UNROLL):
-            lhs = jnp.concatenate([dens_ref[item(i, u, 1)], dens_ref[item(i, u, 2)]], axis=1)
-            near_ref[item(i, u, 0)] += dot(lhs, k_ref[u])
-
+def pair_matrices(list_ref, i, fs_ref, ft_ref, k_ref, at=0):
+    for u in range(UNROLL):
+        x = jnp.concatenate([fs_ref[list_ref[i, (h + 1) * UNROLL + u]] for h in range(2)], axis=0)
+        out = dot(x, ft_ref[list_ref[i, u]])
+        r = lax.rsqrt(out[:, :128])
+        k_ref[at + u] = ((out[:, 128:] * r) * (r * r)).astype(bf16)
+
+
+def pair_apply(list_ref, i, dens_ref, k_ref, near_ref, at=0):
+    for u in range(UNROLL):
+        lhs = jnp.concatenate([dens_ref[list_ref[i, (h + 1) * UNROLL + u]] for h in range(2)], axis=1)
+        near_ref[list_ref[i, u]] += dot(lhs, k_ref[at + u])
+
+
+def near_pairs(list_ref, fs_ref, ft_ref, dens_ref, k_ref, near_ref, start=0):
     def step(i, _):
-        apply(i - 1)
-        matrices(i)
+        pair_apply(list_ref, i - 1, dens_ref, k_ref, near_ref)
+        pair_matrices(list_ref, i, fs_ref, ft_ref, k_ref)
         return 0
 
-    steps = jnp.maximum((list_ref[list_ref.shape[0] - 1, 0] + UNROLL - 1) // UNROLL, 1)
-    matrices(0)
-    lax.fori_loop(1, steps, step, 0)
-    apply(steps - 1)
+    steps = (list_ref[list_ref.shape[0] - 1, 0] + UNROLL - 1) // UNROLL
+    steps = jnp.maximum(steps, start + 1)
+    pair_matrices(list_ref, start, fs_ref, ft_ref, k_ref)
+    lax.fori_loop(start + 1, steps, step, 0)
+    pair_apply(list_ref, steps - 1, dens_ref, k_ref, near_ref)
 
 
 def own_kernel(
-    list_hbm, fs_hbm, ft_hbm, own_ref, near_ref, fs_ref, ft_ref, dens_ref, k_ref, list_ref, sem
+    list_hbm, fs_hbm, ft_hbm, ready_hbm, own_ref,
+    near_ref,
+    fs_ref, ft_ref, ready_ref, dens_ref, k_ref, list_ref, sem,
 ):
-    leaves = fs_hbm.shape[0]
+    leaves = fs_hbm.shape[0] - 1
     half = leaves // 2
     nrhs = 32
     copies = [
-        pltpu.make_async_copy(list_hbm, list_ref, sem.at[3]),
-        pltpu.make_async_copy(fs_hbm, fs_ref.at[pl.ds(0, leaves)], sem.at[0]),
-        pltpu.make_async_copy(ft_hbm, ft_ref.at[pl.ds(0, leaves)], sem.at[1]),
-        pltpu.make_async_copy(fs_hbm.at[0], fs_ref.at[leaves], sem.at[2]),
+        pltpu.make_async_copy(list_hbm, list_ref, sem.at[0]),
+        pltpu.make_async_copy(ready_hbm, ready_ref, sem.at[3]),
+        pltpu.make_async_copy(fs_hbm, fs_ref, sem.at[1]),
+        pltpu.make_async_copy(ft_hbm, ft_ref, sem.at[2]),
     ]
     for c in copies:
         c.start()
@@ -412,9 +423,13 @@
         dens_ref[l] = own_ref[l // half, l % half * nrhs : (l % half + 1) * nrhs, :]
     dens_ref[leaves] = jnp.zeros((nrhs, 128), bf16)
     near_ref[...] = jnp.zeros(near_ref.shape, f32)
-    for c in copies:
+    for c in copies[:2]:
         c.wait()
-    near_pairs(list_ref, fs_ref, ft_ref, dens_ref, k_ref, near_ref)
+    for i in range(AHEAD):
+        pair_apply(list_ref, i, dens_ref, ready_ref, near_ref, i * UNROLL)
+    for c in copies[2:]:
+        c.wait()
+    near_pairs(list_ref, fs_ref, ft_ref, dens_ref, k_ref, near_ref, AHEAD)
 
 
 def leaf_kernel(
@@ -435,7 +450,7 @@
     mine = pl.ds(REACH, leaves)
     copies = [
         pltpu.make_async_copy(fd_own_ref, fd_ref.at[mine], sem.at[0]),
-        pltpu.make_async_copy(ft_hbm, ft_ref.at[pl.ds(0, leaves)], sem.at[1]),
+        pltpu.make_async_copy(ft_hbm, ft_ref, sem.at[1]),
         pltpu.make_async_copy(wf_hbm, wf_ref, sem.at[2]),
         pltpu.make_async_copy(fs_own_ref.at[0], fs_ref.at[wide], sem.at[3]),
         pltpu.make_async_copy(fd_own_ref.at[0], fd_ref.at[wide], sem.at[4]),
@@ -566,7 +581,7 @@
     return pl.BlockSpec(memory_space=pltpu.SMEM)
 
 
-def call(kernel, out, in_specs, scratch, name, flops, vmem_mib, out_specs=None):
+def call(kernel, out, in_specs, scratch, flops, vmem_mib, out_specs=None):
     many = isinstance(out, tuple)
     if out_specs is None:
         out_specs = tuple(vmem() for _ in out) if many else vmem()
@@ -576,7 +591,6 @@
         in_specs=in_specs,
         out_specs=out_specs,
         scratch_shapes=scratch,
-        name=name,
         cost_estimate=pl.CostEstimate(flops=flops, bytes_accessed=1 << 20, transcendentals=0),
         compiler_params=pltpu.CompilerParams(vmem_limit_bytes=vmem_mib << 20),
     )
@@ -589,7 +603,6 @@
         jax.ShapeDtypeStruct((peers, per * nrhs + 8, leaf), bf16),
         [smem(), vmem()],
         [pltpu.SMEM((peers,), jnp.int32), pltpu.SMEM((leaves,), jnp.int32)],
-        "pack",
         1 << 20,
         2,
     )(hbm(leaf_target), hbm(density))
@@ -599,19 +612,19 @@
     leaves, slots = near_list.shape
     nodes = node_points.shape[1] // 64
     nodes_here, node_slots = node_list.shape
-    shape = jax.ShapeDtypeStruct
     return call(
         feature_kernel,
         (
-            pltpu.HBM((leaves, 128, 128), bf16),
+            pltpu.HBM((leaves + 1, 128, 128), bf16),
             pltpu.HBM((leaves, 64, 128), bf16),
-            pltpu.HBM((leaves, 128, 256), bf16),
+            pltpu.HBM((leaves + 1, 128, 256), bf16),
             pltpu.HBM((leaves, 128, 128), bf16),
             pltpu.VMEM((leaves * 24, 128), bf16),
             pltpu.VMEM((nodes_here, node_slots * 32, 128), bf16),
             pltpu.HBM((list_rows(slots, leaves), 128), jnp.int32),
             pltpu.HBM((list_rows(slots, leaves), 128), jnp.int32),
             pltpu.HBM((leaves, 128), jnp.int32),
+            pltpu.HBM((AHEAD * UNROLL, 256, 128), bf16),
         ),
         [smem()] + [vmem()] * 4,
         [
@@ -619,10 +632,11 @@
             pltpu.VMEM((8, nodes * 64), f32),
             pltpu.VMEM((nodes // 2, 128, 128), bf16),
             pltpu.VMEM((nodes_here, 128, 128), bf16),
+            pltpu.SMEM((list_rows(slots, leaves), 128), jnp.int32),
+            pltpu.SemaphoreType.DMA((1,)),
         ],
-        "features",
         1 << 30,
-        14,
+        18,
     )(hbm(node_list), hbm(geometry), hbm(node_points), hbm(near_list.T), hbm(far_list.T))
 
 
@@ -642,7 +656,6 @@
         ),
         [vmem()] * 4,
         [],
-        "skeleton",
         1 << 26,
         6,
     )(
@@ -653,31 +666,30 @@
     )
 
 
-def own_fields(own_list, fs, ft, own):
-    leaves = ft.shape[0]
+def own_fields(own_list, fs, ft, own, ready):
     anywhere = pl.BlockSpec(memory_space=pl.ANY)
     return call(
         own_kernel,
-        pltpu.VMEM((leaves + 1, 32, 128), f32),
-        [anywhere] * 3 + [vmem()],
+        pltpu.VMEM((fs.shape[0], 32, 128), f32),
+        [anywhere] * 4 + [vmem()],
         [
-            pltpu.VMEM((leaves + 1, 128, 128), bf16),
-            pltpu.VMEM((leaves + 1, 128, 256), bf16),
-            pltpu.VMEM((leaves + 1, 32, 128), bf16),
+            pltpu.VMEM(fs.shape, bf16),
+            pltpu.VMEM(ft.shape, bf16),
+            pltpu.VMEM(ready.shape, bf16),
+            pltpu.VMEM((fs.shape[0], 32, 128), bf16),
             pltpu.VMEM((UNROLL, 256, 128), bf16),
             pltpu.SMEM(own_list.shape, jnp.int32),
             pltpu.SemaphoreType.DMA((4,)),
         ],
-        "own",
         1 << 31,
         12,
-    )(hbm(own_list), hbm(fs), hbm(ft), own)
+    )(hbm(own_list), hbm(fs), hbm(ft), hbm(ready), own)
 
 
 def leaf_fields(
     far_slots, halo_list, far_list, node_list, fs, fd, ft, wf, basis_out, transfer, own, got_a, got_b, first, all_skel, gn
 ):
-    leaves = ft.shape[0]
+    leaves = wf.shape[0]
     wide = leaves + 2 * REACH
     nodes = all_skel.shape[0] // 16
     anywhere = pl.BlockSpec(memory_space=pl.ANY)
@@ -710,7 +722,6 @@
             pltpu.SemaphoreType.DMA((12,)),
             pltpu.SemaphoreType.DMA((leaves // FAR_UNROLL,)),
         ],
-        "leaves",
         1 << 31,
         24,
         anywhere,
@@ -731,14 +742,14 @@
     per = density.shape[0] // peers
     outgoing = pack(peers, per, density, leaf_target)
     arrived = lax.all_to_all(outgoing, AXES, split_axis=0, concat_axis=0, tiled=True)
-    fs, fd, ft, wf, split, gn, own_pairs, halo_pairs, far_rows = features(node_list, geometry, node_points, near_list, far_list)
+    fs, fd, ft, wf, split, gn, own_pairs, halo_pairs, far_rows, ready = features(node_list, geometry, node_points, near_list, far_list)
     own, to_a, to_b, node_out = skeletons(arrived, basis_in, transfer, split, per)
-    all_skel = lax.all_to_all(node_out, AXES, split_axis=0, concat_axis=0, tiled=True)
     swap_a = [(i, i ^ 1) for i in range(peers)]
     swap_b = [(i, i + 1) for i in range(1, peers - 1, 2)] + [(i + 1, i) for i in range(1, peers - 1, 2)]
     got_a = lax.ppermute(to_a, AXES, swap_a)
     got_b = lax.ppermute(to_b, AXES, swap_b)
-    first = own_fields(own_pairs, fs, ft, own)
+    all_skel = lax.all_to_all(node_out, AXES, split_axis=0, concat_axis=0, tiled=True)
+    first = own_fields(own_pairs, fs, ft, own, ready)
     return leaf_fields(
         far_list.shape[1], halo_pairs, far_rows, node_list, fs, fd, ft, wf, basis_out, transfer, own, got_a, got_b,
         first, all_skel.reshape(-1, 128), gn,

time: 50.3 us -> 50 us (level)
  the two profiles are of different devices: /device:TPU:1 before, /device:TPU:10 now
where the time goes in v4:
time: 50 us; the launch traced here: 49.6 us
  Pallas kernels  33.7 us (67%)
  starting transfers between devices  15.8 us (32%)
    pallas_call x1, Pallas kernels, leaf_fields(): call(leaf_kernel, jax.ShapeDtypeStruct((leaves, 32, 128), bf16), [anywher...  10.4 us
    pallas_call x1, Pallas kernels, own_fields(): call(own_kernel, pltpu.VMEM((fs.shape[0], 32, 128), f32), [anywhere] * 4...  10.1 us
    pallas_call x1, Pallas kernels, features(): call(feature_kernel, (pltpu.HBM((leaves + 1, 128, 128), bf16), pltpu.HBM(...  9.63 us
    all_to_all x1, starting transfers between devices, on_device(): lax.all_to_all(outgoing, AXES, split_axis=0, concat_axis=0, tiled=True)  6.3 us
    all_to_all x1, starting transfers between devices, on_device(): lax.all_to_all(node_out, AXES, split_axis=0, concat_axis=0, tiled=True)  6.02 us
    ppermute x1, starting transfers between devices, on_device(): got_b = lax.ppermute(to_b, AXES, swap_b)  3.36 us
    pallas_call x1, Pallas kernels, pack(): call(lambda *r: pack_kernel(*r, peers=peers, per=per), jax.ShapeDtypeStru...  1.91 us
    pallas_call x1, Pallas kernels, skeletons(): call(lambda *r: skeleton_kernel(*r, per=per), (pltpu.VMEM((2, rows, 128),...  1.61 us
  transfers between devices with their start and end apart: 4, of which 0 were waited for; matrix products, arithmetic and copies ran while one was open for 0% of the time, Pallas kernels for 40%

profile of v4, /device:TPU:10, one launch (start us, length us, event | category | flops | bytes accessed | tf_op | source)
XLA Modules:
  0.0 49.6 jit_solution(4795168061332893121)
XLA Ops:
  0.0 1.9 %shard_map.101 = bf16[16,72,128]{2,1,0:T(8,128)(2,1)} custom-call(s32[32]{0:T(128)} %r_0_.1, bf16[32,32,128]{2,1,0:T(8,128)(2,1)} %r_1_.1), custom_call_target="tpu_custom_call" | custom-call | flops 1048576 | bytes 1048576 | tf_op jit(solution)/shard_map/pallas_call | solution.py:601
  1.9 6.3 %all-to-all-start = ((bf16[16,72,128]{2,1,0:T(8,128)(2,1)}), bf16[16,72,128]{2,1,0:T(8,128)(2,1)S(1)}, u32[]{:S(2)}, u32[]{:S(2)}) async-start(bf16[16,72,128]{2,1,0:T(8,128)(2,1)} %shard_map.101), calls=%async_computation | async-start | bytes 589824 | tf_op jit(solution)/shard_map/all_to_all | solution.py:744
  8.2 0.0 copy-start
  8.2 0.0 copy-start.1
  8.2 9.6 %shard_map.100 = (bf16[33,128,128]{2,1,0:T(8,128)(2,1)}, bf16[32,64,128]{2,1,0:T(8,128)(2,1)}, bf16[33,128,256]{2,1,0:T(8,128)(2,1)}, bf16[32,128,128]{2,1,0:T(8...) custom-call(s32[4,32]{1,0:T(4,128)} %node_list_hbm.1, ...), custom_call_target="tpu_custom_call" | custom-call | flops 1073741824 | bytes 1048576 | tf_op jit(solution)/shard_map/pallas_call | solution.py:615
  17.9 0.0 all-to-all-done.r_0_
  17.9 0.0 copy-done
  17.9 0.0 copy-done.1
  17.9 1.6 %shard_map.102 = (bf16[2,1152,128]{2,1,0:T(8,128)(2,1)S(1)}, bf16[1152,128]{1,0:T(8,128)(2,1)}, bf16[1152,128]{1,0:T(8,128)(2,1)}, bf16[16,64,128]{2,1,0:T(8,128)(2,1)}) custom-call(bf16[16,72,128]{2,1,0:T(8,128)(2,1)S(1)} %all-to-all-done.r_0_, bf16[16,128,128]{2,1,0:T(8,128)(2,1)S(1)} %bitcast.8, bf16[2,128,512]{2,1,0:T(8,128)(2,1)S(1)} %bitcast.6, ...), custom_call_target="tpu_custom_call" | custom-call | flops 67108864 | bytes 1048576 | tf_op jit(solution)/shard_map/pallas_call | solution.py:649
  19.5 6.0 %all-to-all-start.1 = ((bf16[16,64,128]{2,1,0:T(8,128)(2,1)}), bf16[16,64,128]{2,1,0:T(8,128)(2,1)S(1)}, u32[]{:S(2)}, u32[]{:S(2)}) async-start(bf16[16,64,128]{2,1,0:T(8,128)(2,1)} %get-tuple-element.31), calls=%async_computation.1 | async-start | bytes 524288 | tf_op jit(solution)/shard_map/all_to_all | solution.py:751
  25.5 0.1 collective-permute-start
  25.6 3.4 %collective-permute-start.1 = (bf16[1152,128]{1,0:T(8,128)(2,1)}, bf16[1152,128]{1,0:T(8,128)(2,1)S(1)}, u32[]{:S(2)}, u32[]{:S(2)}) collective-permute-start(bf16[1152,128]{1,0:T(8,128)(2,1)} %get-tuple-element.28), channel_id=1, source_target_pairs={{1,2},{3,4},{5,6},{7,8},{9,10},{11,12},{13,14},{2,1},{4,3},{6,5},{... | collective-permute-start | bytes 884744 | tf_op jit(solution)/shard_map/ppermute | solution.py:750
  29.0 10.1 %shard_map.103.first_ref = f32[33,32,128]{2,1,0:T(8,128)S(1)} custom-call(s32[25,128]{1,0:T(8,128)} %get-tuple-element.29.list_hbm, bf16[33,128,128]{2,1,0:T(8,128)(2,1)} %get-tuple-element.21.fs_hbm.fs_own_ref, bf16[33,128,256]{2,1,0:T(8,128)(2,1)} %get-tuple-element.23.ft_hbm, bf16[24,256,128]{2,1,0:T(8,128)(2,1)} %get-tuple-element.30.ready_hbm, ...), custom_call_target="tpu_custom_call" | custom-call | flops 2147483648 | bytes 1048576 | tf_op jit(solution)/shard_map/pallas_call | solution.py:671
  39.1 0.0 collective-permute-done.a_any
  39.1 0.0 collective-permute-done.1.b_any
  39.1 0.0 all-to-all-done.1
  39.2 10.4 %shard_map.104 = bf16[32,32,128]{2,1,0:T(8,128)(2,1)} custom-call(s32[25,128]{1,0:T(8,128)} %get-tuple-element.19.list_hbm, s32[32,128]{1,0:T(8,128)} %get-tuple-element.20.far_list_hbm, s32[4,32]{1,0:T(4,128)} %node_list_hbm.1, bf16[33,128,128]{2,1,0:T(8,128)(2,1)} %get-tuple-element.21.fs_hbm.fs_own_ref, ...), custom_call_target="tpu_custom_call" | custom-call | flops 2147483648 | bytes 1048576 | tf_op jit(solution)/shard_map/pallas_call | solution.py:697
Async XLA Ops:
  1.9 16.0 %all-to-all-start = ((bf16[16,72,128]{2,1,0:T(8,128)(2,1)}), bf16[16,72,128]{2,1,0:T(8,128)(2,1)S(1)}, u32[]{:S(2)}, u32[]{:S(2)}) async-start(bf16[16,72,128]{2,1,0:T(8,128)(2,1)} %shard_map.101), calls=%async_computation | async-start | bytes 589824 | tf_op jit(solution)/shard_map/all_to_all | solution.py:744
  8.2 9.7 %copy-start = (bf16[4,64,512]{2,1,0:T(8,128)(2,1)S(1)}, bf16[4,64,512]{2,1,0:T(8,128)(2,1)}, u32[]{:S(2)}) copy-start(bf16[4,64,512]{2,1,0:T(8,128)(2,1)} %transfer_hbm.1) | copy-start | bytes 786436
  8.2 9.7 %copy-start.1 = (bf16[32,64,128]{2,1,0:T(8,128)(2,1)S(1)}, bf16[32,64,128]{2,1,0:T(8,128)(2,1)}, u32[]{:S(2)}) copy-start(bf16[32,64,128]{2,1,0:T(8,128)(2,1)} %param.16) | copy-start | bytes 1572868
  19.5 19.7 %all-to-all-start.1 = ((bf16[16,64,128]{2,1,0:T(8,128)(2,1)}), bf16[16,64,128]{2,1,0:T(8,128)(2,1)S(1)}, u32[]{:S(2)}, u32[]{:S(2)}) async-start(bf16[16,64,128]{2,1,0:T(8,128)(2,1)} %get-tuple-element.31), calls=%async_computation.1 | async-start | bytes 524288 | tf_op jit(solution)/shard_map/all_to_all | solution.py:751
  25.5 13.6 %collective-permute-start = (bf16[1152,128]{1,0:T(8,128)(2,1)}, bf16[1152,128]{1,0:T(8,128)(2,1)S(1)}, u32[]{:S(2)}, u32[]{:S(2)}) collective-permute-start(bf16[1152,128]{1,0:T(8,128)(2,1)} %get-tuple-element.27), channel_id=1, source_target_pairs={{0,1},{1,0},{2,3},{3,2},{4,5},{5,4},{6,7},{7,6},{8,9},{9,8},{10,11... | collective-permute-start | bytes 884744 | tf_op jit(solution)/shard_map/ppermute | solution.py:749
  25.6 13.5 %collective-permute-start.1 = (bf16[1152,128]{1,0:T(8,128)(2,1)}, bf16[1152,128]{1,0:T(8,128)(2,1)S(1)}, u32[]{:S(2)}, u32[]{:S(2)}) collective-permute-start(bf16[1152,128]{1,0:T(8,128)(2,1)} %get-tuple-element.28), channel_id=1, source_target_pairs={{1,2},{3,4},{5,6},{7,8},{9,10},{11,12},{13,14},{2,1},{4,3},{6,5},{... | collective-permute-start | bytes 884744 | tf_op jit(solution)/shard_map/ppermute | solution.py:750
